TPU v7x, 32 devices: a whole 2x2x4 slice. The times are simulated.
32 devices in a mesh: dp: 2 (over x), row: 4 (over y, core), col: 4 (over z).
Axes of the slice: x: 2, y: 2, z: 4, core: 2. Of those that a mesh axis runs over, the one named last changes fastest.
Arguments:
- tokens: bfloat16 [8, 64, 64, 768], P('dp', 'row', 'col'), may hold values from -6 to 6
- cls_token: bfloat16 [8, 768], P('dp'), may hold values from -6 to 6
- patch_mask: int32 [8, 64, 64], P('dp', 'row', 'col'), may hold values from 0 to 1, as said below
- loss_mask: int32 [8, 64, 64], P('dp', 'row', 'col'), may hold values 0 or 1
- mask_emb: float32 [768], replicated, may hold values from -5 to 5
- ln1_gain: float32 [768], replicated, may hold values from 0.5 to 1.5
- ln1_bias: float32 [768], replicated, may hold values from -1.5 to 1.5
- w_qkv: bfloat16 [768, 2304], replicated, may hold values from -0.21875 to 0.21875
- q_bias: float32 [768], replicated, may hold values from -2.5 to 2.5
- v_bias: float32 [768], replicated, may hold values from -2.5 to 2.5
- rel_table: float32 [12, 50], replicated, may hold values from -4 to 4
- w_out: bfloat16 [768, 768], replicated, may hold values from -0.875 to 0.875
- out_bias: float32 [768], replicated, may hold values from -1.5 to 1.5
- scale_attn: float32 [768], replicated, may hold values from 0.25 to 1.75
- ln2_gain: float32 [768], replicated, may hold values from 0.5 to 1.5
- ln2_bias: float32 [768], replicated, may hold values from -1.5 to 1.5
- w_up: bfloat16 [768, 3072], replicated, may hold values from -0.21875 to 0.21875
- up_bias: float32 [3072], replicated, may hold values from -2.5 to 2.5
- w_down: bfloat16 [3072, 768], replicated, may hold values from -0.109375 to 0.109375
- down_bias: float32 [768], replicated, may hold values from -1.5 to 1.5
- scale_mlp: float32 [768], replicated, may hold values from 0.25 to 1.75
- out_grad: bfloat16 [8, 64, 64, 768], P('dp', 'row', 'col'), may hold values from -6 to 6
Outputs:
- out: bfloat16 [8, 64, 64, 768], P('dp', 'row', 'col')
- out_cls: bfloat16 [8, 768], P('dp')
- d_tokens: float32 [8, 64, 64, 768], P('dp', 'row', 'col')
- d_cls: float32 [8, 768], P('dp')
- d_w_qkv: float32 [768, 2304], P(('row', 'col'), 'dp')
- d_w_out: float32 [768, 768], P(('row', 'col'), 'dp')
- d_w_up: float32 [768, 3072], P(('row', 'col'), 'dp')
- d_w_down: float32 [3072, 768], P(('row', 'col'), 'dp')
- d_mask_emb: float32 [768], replicated
- d_ln1_gain: float32 [768], replicated
- d_ln1_bias: float32 [768], replicated
- d_q_bias: float32 [768], replicated
- d_v_bias: float32 [768], replicated
- d_rel_table: float32 [12, 50], replicated
- d_out_bias: float32 [768], replicated
- d_scale_attn: float32 [768], replicated
- d_ln2_gain: float32 [768], replicated
- d_ln2_bias: float32 [768], replicated
- d_up_bias: float32 [3072], replicated
- d_down_bias: float32 [768], replicated
- d_scale_mlp: float32 [768], replicated
Inputs may be any that keep to these rules, and one draw needn't show every extreme that they name: `patch_mask`: 1 marks a patch that is replaced by the mask embedding. Each page draws its own rate of ones, from 20 to 60 percent. `loss_mask`: 1 marks a patch whose loss counts where it is masked.
All inputs are finite; a program needn't handle non-finite values. No bound on the sum of `loss_mask` on one device may be relied on, other than what follows from the above.
Results may differ from a plain program's by a relative error of at most 0.012.
Values may be sent and summed in bfloat16 or wider, within the bound.
No kernel may reach another device: no remote copies, remote signals or barrier semaphores. Data moves between devices by JAX's collectives and lax.ppermute only.
A program may use at most 832 MiB of HBM per device.

v0:
```python
import math

import jax
import jax.numpy as jnp
from jax import lax
from jax.sharding import PartitionSpec as P


def passed_along(value, axis, steps):
    count = lax.axis_size(axis)
    first, last = (max(0, -steps), min(count, count - steps))
    return lax.ppermute(value, axis, [(source, source + steps) for source in range(first, last)])


def extended(array, sides, width):
    for axis, dim in sides:
        peers, length = (lax.axis_size(axis), array.shape[dim])
        up = [(i, (i + 1) % peers) for i in range(peers - 1)]
        down = [(j, i) for i, j in up]
        last = lax.slice_in_dim(array, length - width, length, axis=dim)
        first = lax.slice_in_dim(array, 0, width, axis=dim)
        before = lax.ppermute(last, axis, up)
        after = lax.ppermute(first, axis, down)
        array = jnp.concatenate([before, array, after], axis=dim)
    return array


def combined_all(part, axis, combine):
    gathered = jax.tree.map(lambda a: lax.all_gather(a, axis), part)

    def take(source):
        return jax.tree.map(lambda a: lax.dynamic_index_in_dim(a, source, 0, False), gathered)

    return lax.fori_loop(
        1, lax.axis_size(axis), lambda source, state: combine(state, take(source)), take(0)
    )


def norm_forward(inputs, norm_gain, norm_bias):
    row_mean = jnp.mean(inputs, axis=-1, keepdims=True)
    centred = inputs - row_mean
    inv_std = lax.rsqrt(jnp.mean(centred * centred, axis=-1, keepdims=True) + 1e-06)
    unit_rows = centred * inv_std
    return (unit_rows * norm_gain + norm_bias, unit_rows, inv_std)


def norm_backward(incoming, unit_rows, inv_std, norm_gain):
    scaled = incoming * norm_gain
    centred = scaled - jnp.mean(scaled, axis=-1, keepdims=True)
    outgoing = inv_std * (
        centred - unit_rows * jnp.mean(scaled * unit_rows, axis=-1, keepdims=True)
    )
    return (outgoing, jnp.sum(incoming * unit_rows, axis=0), jnp.sum(incoming, axis=0))


def merge_parts(first_part, second_part):
    first_top, first_sum, first_acc = first_part
    second_top, second_sum, second_acc = second_part
    joint_top = jnp.maximum(first_top, second_top)
    first_weight = jnp.exp(first_top - joint_top)
    second_weight = jnp.exp(second_top - joint_top)
    joint_sum = first_sum * first_weight + second_sum * second_weight
    joint_acc = first_acc * first_weight[..., None] + second_acc * second_weight[..., None]
    return (joint_top, joint_sum, joint_acc)


def window_slice(array, shift_r, shift_c, tile_rows, tile_cols):
    return array[:, shift_r : shift_r + tile_rows, shift_c : shift_c + tile_cols]


def matmul(left_op, right_op):
    return jnp.dot(left_op, right_op, preferred_element_type=jnp.float32)


def contract_rows(left_op, right_op):
    return jnp.einsum("ra,rb->ab", left_op, right_op, preferred_element_type=jnp.float32)


def times_transposed(left_op, right_op):
    return jnp.einsum("ra,ba->rb", left_op, right_op, preferred_element_type=jnp.float32)


def rims_back(padded, tile_rows, tile_cols):
    left_edge = padded[:, :, :3]
    right_edge = padded[:, :, tile_cols + 3 :]
    from_left = passed_along(right_edge, "col", 1)
    from_right = passed_along(left_edge, "col", -1)
    middle = padded[:, :, 3 : tile_cols + 3]
    middle = middle.at[:, :, :3].add(from_left)
    middle = middle.at[:, :, tile_cols - 3 :].add(from_right)
    top_edge = middle[:, :3]
    bottom_edge = middle[:, tile_rows + 3 :]
    from_above = passed_along(bottom_edge, "row", 1)
    from_below = passed_along(top_edge, "row", -1)
    inner = middle[:, 3 : tile_rows + 3]
    inner = inner.at[:, :3].add(from_above)
    return inner.at[:, tile_rows - 3 :].add(from_below)


def shards(
    tokens,
    cls_token,
    patch_mask,
    loss_mask,
    mask_emb,
    ln1_gain,
    ln1_bias,
    w_qkv,
    q_bias,
    v_bias,
    rel_table,
    w_out,
    out_bias,
    scale_attn,
    ln2_gain,
    ln2_bias,
    w_up,
    up_bias,
    w_down,
    down_bias,
    scale_mlp,
    out_grad,
):
    page_count, tile_rows, tile_cols, model_width = tokens.shape
    head_count = rel_table.shape[0]
    head_width = model_width // head_count
    row_count = page_count * tile_rows * tile_cols
    score_scale = 1.0 / math.sqrt(head_width)
    grid_rows = tile_rows * lax.axis_size("row")
    grid_cols = tile_cols * lax.axis_size("col")
    row_place = lax.axis_index("row") * tile_rows - 3 + jnp.arange(tile_rows + 6)
    col_place = lax.axis_index("col") * tile_cols - 3 + jnp.arange(tile_cols + 6)
    inside = ((row_place >= 0) & (row_place < grid_rows))[:, None] & (
        (col_place >= 0) & (col_place < grid_cols)
    )[None, :]
    is_leader = ((lax.axis_index("row") == 0) & (lax.axis_index("col") == 0)).astype(jnp.float32)
    shape_four = (page_count, tile_rows, tile_cols, head_count, head_width)
    shape_pad = (page_count, tile_rows + 6, tile_cols + 6, head_count, head_width)
    masked = (patch_mask == 1).reshape(row_count, 1)
    swapped = jnp.where(
        masked, mask_emb, tokens.astype(jnp.float32).reshape(row_count, model_width)
    )
    normed_full, unit_one, inv_one = norm_forward(swapped, ln1_gain, ln1_bias)
    normed = normed_full.astype(jnp.bfloat16)
    projected = matmul(normed, w_qkv)
    query_rows = (projected[:, :model_width] + q_bias).astype(jnp.bfloat16)
    key_rows = projected[:, model_width : 2 * model_width].astype(jnp.bfloat16)
    value_rows = (projected[:, 2 * model_width :] + v_bias).astype(jnp.bfloat16)
    class_in = cls_token.astype(jnp.float32)
    class_full, class_unit, class_inv = norm_forward(class_in, ln1_gain, ln1_bias)
    class_normed = class_full.astype(jnp.bfloat16)
    class_proj = matmul(class_normed, w_qkv)
    class_query = (
        (class_proj[:, :model_width] + q_bias)
        .astype(jnp.bfloat16)
        .reshape(page_count, head_count, head_width)
    )
    class_key = (
        class_proj[:, model_width : 2 * model_width]
        .astype(jnp.bfloat16)
        .reshape(page_count, head_count, head_width)
    )
    class_value = (
        (class_proj[:, 2 * model_width :] + v_bias)
        .astype(jnp.bfloat16)
        .reshape(page_count, head_count, head_width)
    )
    key_value = jnp.concatenate([key_rows, value_rows], axis=-1).reshape(
        page_count, tile_rows, tile_cols, 2 * model_width
    )
    padded = extended(key_value, (("row", 1), ("col", 2)), 3)
    key_pad = padded[..., :model_width].reshape(shape_pad)
    value_pad = padded[..., model_width:].reshape(shape_pad)
    query_four = query_rows.reshape(shape_four)
    score_list = []
    for shift_r in range(7):
        for shift_c in range(7):
            key_part = window_slice(key_pad, shift_r, shift_c, tile_rows, tile_cols)
            raw_score = jnp.einsum(
                "pijhd,pijhd->pijh", query_four, key_part, preferred_element_type=jnp.float32
            )
            score_val = raw_score * score_scale + rel_table[:, shift_r * 7 + shift_c]
            window_ok = inside[shift_r : shift_r + tile_rows, shift_c : shift_c + tile_cols][
                None, :, :, None
            ]
            score_list.append(jnp.where(window_ok, score_val, -1e30))
    raw_score = jnp.einsum(
        "pijhd,phd->pijh", query_four, class_key, preferred_element_type=jnp.float32
    )
    score_list.append(raw_score * score_scale + rel_table[:, 49])
    scores = jnp.stack(score_list, axis=-1)
    row_top = jnp.max(scores, axis=-1, keepdims=True)
    exp_terms = jnp.exp(scores - row_top)
    exp_total = jnp.sum(exp_terms, axis=-1, keepdims=True)
    prob_full = exp_terms / exp_total
    kept_probs = prob_full.astype(jnp.bfloat16)
    mixed = kept_probs[..., 49, None].astype(jnp.float32) * class_value[:, None, None].astype(
        jnp.float32
    )
    for shift_r in range(7):
        for shift_c in range(7):
            value_part = window_slice(value_pad, shift_r, shift_c, tile_rows, tile_cols)
            mixed = mixed + kept_probs[..., shift_r * 7 + shift_c, None].astype(
                jnp.float32
            ) * value_part.astype(jnp.float32)
    key_three = key_rows.reshape(page_count, tile_rows * tile_cols, head_count, head_width)
    value_three = value_rows.reshape(page_count, tile_rows * tile_cols, head_count, head_width)
    class_raw = (
        jnp.einsum("phd,pnhd->phn", class_query, key_three, preferred_element_type=jnp.float32)
        * score_scale
    )
    local_top = jnp.max(class_raw, axis=-1)
    local_exp = jnp.exp(class_raw - local_top[..., None])
    local_sum = jnp.sum(local_exp, axis=-1)
    local_acc = jnp.einsum(
        "phn,pnhd->phd",
        local_exp,
        value_three.astype(jnp.float32),
        preferred_element_type=jnp.float32,
    )
    merged = combined_all((local_top, local_sum, local_acc), ("row", "col"), merge_parts)
    self_score = (
        jnp.sum(class_query.astype(jnp.float32) * class_key.astype(jnp.float32), axis=-1)
        * score_scale
    )
    merged = merge_parts(
        merged, (self_score, jnp.ones_like(self_score), class_value.astype(jnp.float32))
    )
    class_mixed = (
        (merged[2] / merged[1][..., None]).reshape(page_count, model_width).astype(jnp.bfloat16)
    )
    attended = mixed.reshape(row_count, model_width).astype(jnp.bfloat16)
    branch = matmul(attended, w_out) + out_bias
    residual = swapped + scale_attn * branch
    normed_two_full, unit_two, inv_two = norm_forward(residual, ln2_gain, ln2_bias)
    normed_two = normed_two_full.astype(jnp.bfloat16)
    hidden = matmul(normed_two, w_up) + up_bias
    activated = jax.nn.gelu(hidden, approximate=False).astype(jnp.bfloat16)
    mlp_out = matmul(activated, w_down) + down_bias
    block_out = residual + scale_mlp * mlp_out
    out = block_out.reshape(page_count, tile_rows, tile_cols, model_width).astype(jnp.bfloat16)
    class_branch = matmul(class_mixed, w_out) + out_bias
    class_resid = class_in + scale_attn * class_branch
    class_two = norm_forward(class_resid, ln2_gain, ln2_bias)[0].astype(jnp.bfloat16)
    class_hidden = jax.nn.gelu(matmul(class_two, w_up) + up_bias, approximate=False).astype(
        jnp.bfloat16
    )
    out_cls = (class_resid + scale_mlp * (matmul(class_hidden, w_down) + down_bias)).astype(
        jnp.bfloat16
    )
    loss_weight = (patch_mask * loss_mask).reshape(row_count, 1).astype(jnp.float32)
    grad_out = out_grad.astype(jnp.float32).reshape(row_count, model_width) * loss_weight
    grad_scale_mlp = jnp.sum(grad_out * mlp_out, axis=0)
    grad_mlp = (scale_mlp * grad_out).astype(jnp.bfloat16)
    grad_down_bias = jnp.sum(grad_mlp.astype(jnp.float32), axis=0)
    grad_down = contract_rows(activated, grad_mlp)
    grad_act = times_transposed(grad_mlp, w_down)
    gelu_value, gelu_pull = jax.vjp(lambda inner: jax.nn.gelu(inner, approximate=False), hidden)
    grad_hidden = gelu_pull(grad_act)[0].astype(jnp.bfloat16)
    grad_up_bias = jnp.sum(grad_hidden.astype(jnp.float32), axis=0)
    grad_up = contract_rows(normed_two, grad_hidden)
    grad_norm_two = times_transposed(grad_hidden, w_up)
    norm_two_back, grad_ln2_gain, grad_ln2_bias = norm_backward(
        grad_norm_two, unit_two, inv_two, ln2_gain
    )
    grad_residual = grad_out + norm_two_back
    grad_scale_attn = jnp.sum(grad_residual * branch, axis=0)
    grad_branch = (scale_attn * grad_residual).astype(jnp.bfloat16)
    grad_out_bias = jnp.sum(grad_branch.astype(jnp.float32), axis=0)
    grad_wout = contract_rows(attended, grad_branch)
    grad_mixed = times_transposed(grad_branch, w_out).astype(jnp.bfloat16).reshape(shape_four)
    dprob_list = []
    for shift_r in range(7):
        for shift_c in range(7):
            value_part = window_slice(value_pad, shift_r, shift_c, tile_rows, tile_cols)
            dprob_list.append(
                jnp.einsum(
                    "pijhd,pijhd->pijh", grad_mixed, value_part, preferred_element_type=jnp.float32
                )
            )
    dprob_list.append(
        jnp.einsum("pijhd,phd->pijh", grad_mixed, class_value, preferred_element_type=jnp.float32)
    )
    dprob = jnp.stack(dprob_list, axis=-1)
    row_delta = jnp.sum(prob_full * dprob, axis=-1, keepdims=True)
    dscore = prob_full * (dprob - row_delta)
    grad_table = jnp.sum(dscore, axis=(0, 1, 2))
    dscore_low = (dscore * score_scale).astype(jnp.bfloat16)
    query_grad = dscore_low[..., 49, None].astype(jnp.float32) * class_key[:, None, None].astype(
        jnp.float32
    )
    for shift_r in range(7):
        for shift_c in range(7):
            key_part = window_slice(key_pad, shift_r, shift_c, tile_rows, tile_cols)
            query_grad = query_grad + dscore_low[..., shift_r * 7 + shift_c, None].astype(
                jnp.float32
            ) * key_part.astype(jnp.float32)
    class_key_part = jnp.einsum(
        "pijh,pijhd->phd", dscore_low[..., 49], query_four, preferred_element_type=jnp.float32
    )
    class_value_part = jnp.einsum(
        "pijh,pijhd->phd", kept_probs[..., 49], grad_mixed, preferred_element_type=jnp.float32
    )
    key_grad_pad = jnp.zeros(shape_pad, jnp.float32)
    value_grad_pad = jnp.zeros(shape_pad, jnp.float32)
    query_wide = query_four.astype(jnp.float32)
    grad_wide = grad_mixed.astype(jnp.float32)
    for shift_r in range(7):
        for shift_c in range(7):
            offset_id = shift_r * 7 + shift_c
            key_term = dscore_low[..., offset_id, None].astype(jnp.float32) * query_wide
            value_term = kept_probs[..., offset_id, None].astype(jnp.float32) * grad_wide
            key_grad_pad = key_grad_pad.at[
                :, shift_r : shift_r + tile_rows, shift_c : shift_c + tile_cols
            ].add(key_term)
            value_grad_pad = value_grad_pad.at[
                :, shift_r : shift_r + tile_rows, shift_c : shift_c + tile_cols
            ].add(value_term)
    flat_pad = (page_count, tile_rows + 6, tile_cols + 6, model_width)
    joined = jnp.concatenate(
        [key_grad_pad.reshape(flat_pad), value_grad_pad.reshape(flat_pad)], axis=-1
    )
    own_grads = rims_back(joined, tile_rows, tile_cols)
    key_grad = own_grads[..., :model_width]
    value_grad = own_grads[..., model_width:]
    query_low = query_grad.reshape(row_count, model_width).astype(jnp.bfloat16)
    key_low = key_grad.reshape(row_count, model_width).astype(jnp.bfloat16)
    value_low = value_grad.reshape(row_count, model_width).astype(jnp.bfloat16)
    class_dk, class_dv = lax.psum((class_key_part, class_value_part), ("row", "col"))
    class_key_low = class_dk.reshape(page_count, model_width).astype(jnp.bfloat16)
    class_value_low = class_dv.reshape(page_count, model_width).astype(jnp.bfloat16)
    grad_proj = jnp.concatenate([query_low, key_low, value_low], axis=-1)
    class_grad_proj = jnp.concatenate(
        [jnp.zeros((page_count, model_width), jnp.bfloat16), class_key_low, class_value_low],
        axis=-1,
    )
    grad_qkv = contract_rows(normed, grad_proj) + is_leader * contract_rows(
        class_normed, class_grad_proj
    )
    grad_q_bias = jnp.sum(query_low.astype(jnp.float32), axis=0)
    grad_v_bias = jnp.sum(value_low.astype(jnp.float32), axis=0) + is_leader * jnp.sum(
        class_value_low.astype(jnp.float32), axis=0
    )
    grad_normed = times_transposed(grad_proj, w_qkv)
    norm_one_back, grad_ln1_gain, grad_ln1_bias = norm_backward(
        grad_normed, unit_one, inv_one, ln1_gain
    )
    grad_sequence = grad_residual + norm_one_back
    class_grad_normed = times_transposed(class_grad_proj, w_qkv)
    d_cls, class_gain_grad, class_bias_grad = norm_backward(
        class_grad_normed, class_unit, class_inv, ln1_gain
    )
    grad_ln1_gain = grad_ln1_gain + is_leader * class_gain_grad
    grad_ln1_bias = grad_ln1_bias + is_leader * class_bias_grad
    d_tokens = jnp.where(masked, 0.0, grad_sequence).reshape(
        page_count, tile_rows, tile_cols, model_width
    )
    grad_emb = jnp.sum(jnp.where(masked, grad_sequence, 0.0), axis=0)
    bundle = (grad_qkv, grad_wout, grad_up, grad_down)
    partial_grads = (
        lax.psum_scatter(bundle[0], ("row", "col"), scatter_dimension=0, tiled=True),
        lax.psum_scatter(bundle[1], ("row", "col"), scatter_dimension=0, tiled=True),
        lax.psum_scatter(bundle[2], ("row", "col"), scatter_dimension=0, tiled=True),
        lax.psum_scatter(bundle[3], ("row", "col"), scatter_dimension=0, tiled=True),
    )
    weight_grads = (
        lax.psum_scatter(partial_grads[0], "dp", scatter_dimension=1, tiled=True),
        lax.psum_scatter(partial_grads[1], "dp", scatter_dimension=1, tiled=True),
        lax.psum_scatter(partial_grads[2], "dp", scatter_dimension=1, tiled=True),
        lax.psum_scatter(partial_grads[3], "dp", scatter_dimension=1, tiled=True),
    )
    small_sums = lax.psum(
        (
            grad_emb,
            grad_ln1_gain,
            grad_ln1_bias,
            grad_q_bias,
            grad_v_bias,
            grad_table,
            grad_out_bias,
            grad_scale_attn,
            grad_ln2_gain,
            grad_ln2_bias,
            grad_up_bias,
            grad_down_bias,
            grad_scale_mlp,
        ),
        ("dp", "row", "col"),
    )
    return (
        out,
        out_cls,
        d_tokens,
        d_cls,
        weight_grads[0],
        weight_grads[1],
        weight_grads[2],
        weight_grads[3],
        small_sums[0],
        small_sums[1],
        small_sums[2],
        small_sums[3],
        small_sums[4],
        small_sums[5],
        small_sums[6],
        small_sums[7],
        small_sums[8],
        small_sums[9],
        small_sums[10],
        small_sums[11],
        small_sums[12],
    )


def solution(mesh):
    placed = (
        P("dp", "row", "col", None),
        P("dp", None),
        P("dp", "row", "col"),
        P("dp", "row", "col"),
        P(),
        P(),
        P(),
        P(),
        P(),
        P(),
        P(),
        P(),
        P(),
        P(),
        P(),
        P(),
        P(),
        P(),
        P(),
        P(),
        P(),
        P("dp", "row", "col", None),
    )
    return jax.shard_map(
        shards,
        mesh=mesh,
        in_specs=placed,
        out_specs=(
            P("dp", "row", "col", None),
            P("dp", None),
            P("dp", "row", "col", None),
            P("dp", None),
            P(("row", "col"), "dp"),
            P(("row", "col"), "dp"),
            P(("row", "col"), "dp"),
            P(("row", "col"), "dp"),
            P(),
            P(),
            P(),
            P(),
            P(),
            P(),
            P(),
            P(),
            P(),
            P(),
            P(),
            P(),
            P(),
        ),
        check_vma=False,
    )
```

profile of v0, /device:TPU:0, one launch (start us, length us, event | category | flops | bytes accessed | tf_op | source)
XLA Modules:
  0.0 3091.5 jit_solution(14129959861412292912)
XLA Ops:
  115.1 32.2 %fusion.641 = (bf16[4,16,16,12,64]{4,3,0,2,1:T(8,128)(2,1)}, bf16[4,16,16,12,64]{4,3,0,2,1:T(8,128)(2,1)}, bf16[4,16,16,12,64]{4,3,0,2,1:T(8,128)(2,1)}, bf16[4,...) fusion(bf16[4,22,22,12,64]{4,3,0,2,1:T(8,128)(2,1)} %reshape.4943), kind=kLoop, calls=%fused_computation.1387 | loop fusion | bytes 34603008 | tf_op jit(solution)/shard_map/slice | solution.py:68
  147.3 52.2 %fusion.640 = (bf16[4,16,16,12,64]{4,3,0,2,1:T(8,128)(2,1)}, bf16[4,16,16,12,64]{4,3,0,2,1:T(8,128)(2,1)}, bf16[4,16,16,12,64]{4,3,0,2,1:T(8,128)(2,1)}, bf16[4,...) fusion(bf16[4,22,22,12,64]{4,3,0,2,1:T(8,128)(2,1)} %reshape.4943), kind=kLoop, calls=%fused_computation.1386 | loop fusion | bytes 59768832 | tf_op jit(solution)/shard_map/slice | solution.py:68
  199.5 24.9 fusion.639
  224.4 48.5 %fusion.167 = (f32[4,16,16,12]{3,2,1,0:T(8,128)}, f32[4,16,16,12]{3,2,1,0:T(8,128)}, f32[4,16,16,12]{3,2,1,0:T(8,128)}, f32[4,16,16,12]{3,2,1,0:T(8,128)}, f32[4...) fusion(bf16[4,16,16,12,64]{4,3,2,1,0:T(8,128)(2,1)} %reshape.49, ...), kind=kLoop, calls=%fused_computation.492 | loop fusion | flops 43032576 | bytes 30769152
  313.9 35.9 %fusion.165 = (f32[4,16,16,12]{3,2,1,0:T(8,128)}, f32[4,16,16,12]{3,2,1,0:T(8,128)}, f32[4,16,16,12]{3,2,1,0:T(8,128)}, f32[4,16,16,12]{3,2,1,0:T(8,128)}, f32[4...) fusion(bf16[4,16,16,12,64]{4,3,2,1,0:T(8,128)(2,1)} %reshape.49, ...), kind=kLoop, calls=%fused_computation.490 | loop fusion | flops 31297536 | bytes 22659072
  379.5 48.8 %fusion.166 = (f32[4,16,16,12]{3,2,1,0:T(8,128)}, f32[4,16,16,12]{3,2,1,0:T(8,128)}, f32[4,16,16,12]{3,2,1,0:T(8,128)}, f32[4,16,16,12]{3,2,1,0:T(8,128)}, f32[4...) fusion(bf16[4,16,16,12,64]{4,3,2,1,0:T(8,128)(2,1)} %reshape.49, ...), kind=kLoop, calls=%fused_computation.491 | loop fusion | flops 43032576 | bytes 30769152
  558.1 11.4 fusion.4
  597.4 32.2 %fusion.638 = (bf16[4,16,16,12,64]{4,3,0,2,1:T(8,128)(2,1)}, bf16[4,16,16,12,64]{4,3,0,2,1:T(8,128)(2,1)}, bf16[4,16,16,12,64]{4,3,0,2,1:T(8,128)(2,1)}, bf16[4,...) fusion(bf16[4,22,22,12,64]{4,3,0,2,1:T(8,128)(2,1)} %reshape.4945), kind=kLoop, calls=%fused_computation.1384 | loop fusion | bytes 34603008 | tf_op jit(solution)/shard_map/slice | solution.py:68
  629.6 52.1 %fusion.637 = (bf16[4,16,16,12,64]{4,3,0,2,1:T(8,128)(2,1)}, bf16[4,16,16,12,64]{4,3,0,2,1:T(8,128)(2,1)}, bf16[4,16,16,12,64]{4,3,0,2,1:T(8,128)(2,1)}, bf16[4,...) fusion(bf16[4,22,22,12,64]{4,3,0,2,1:T(8,128)(2,1)} %reshape.4945), kind=kLoop, calls=%fused_computation.1383 | loop fusion | bytes 59768832 | tf_op jit(solution)/shard_map/slice | solution.py:68
  681.8 25.4 fusion.636
  819.5 159.9 %fusion.390 = bf16[4,16,16,12,64]{4,3,2,1,0:T(8,128)(2,1)} fusion(f32[4,16,16,12]{3,2,1,0:T(8,128)} %copy.917, f32[4,16,16,12]{3,2,1,0:T(8,128)} %copy.915, f32[4,16,16,12]{3,2,1,0:T(8,128)} %copy.913, f32[4,16,16,12]{3,2,1,0:T(8,128)} %copy.911, f32[4,16,16,12]{3,2,1,0:T(8,128)} %copy.909, f32[4,16,16,12]{3,2,1,0:T(8,128)} %copy.907, ...), kind=kLoop, calls=%fused_computation.716 | loop fusion | flops 117178368 | bytes 81113088 | tf_op jit(solution)/shard_map/convert_element_type | solution.py:232
  991.5 36.4 %multiply_convert_fusion.1 = (bf16[1024,3072]{1,0:T(8,128)(2,1)}, f32[1024,3072]{1,0:T(8,128)}, f32[1024,3072]{1,0:T(8,128)}) fusion(f32[3072]{0:T(1024)S(1)} %copy-done.286, bf16[768,3072]{1,0:T(8,128)(2,1)} %param.244, f32[1024,768]{1,0:T(8,128)S(1)} %get-tuple-element.1702, f32[768]{0:T(1024)S(1)} %copy-done.230, f32[768]{0:T(1024)S(1)} %copy-done.229, ...), kind=kOutput, calls=%fused_computation.224 | convolution fusion | flops 5043388416 | bytes 39348224 | tf_op jit(solution)/shard_map/dot_general | solution.py:72
  1028.0 19.2 convert_reduce_fusion
  1079.8 48.6 %fusion.301 = (f32[4,16,16,12]{3,2,1,0:T(8,128)}, f32[4,16,16,12]{3,2,1,0:T(8,128)}, f32[4,16,16,12]{3,2,1,0:T(8,128)}, f32[4,16,16,12]{3,2,1,0:T(8,128)}, f32[4...) fusion(bf16[4,16,16,12,64]{4,3,2,1,0:T(8,128)(2,1)} %reshape.49, ...), kind=kLoop, calls=%fused_computation.626 | loop fusion | flops 43032576 | bytes 30769152
  1128.4 48.7 %fusion.302 = (f32[4,16,16,12]{3,2,1,0:T(8,128)}, f32[4,16,16,12]{3,2,1,0:T(8,128)}, f32[4,16,16,12]{3,2,1,0:T(8,128)}, f32[4,16,16,12]{3,2,1,0:T(8,128)}, f32[4...) fusion(bf16[4,16,16,12,64]{4,3,2,1,0:T(8,128)(2,1)} %reshape.49, ...), kind=kLoop, calls=%fused_computation.627 | loop fusion | flops 43032576 | bytes 30769152
  1177.1 39.4 %fusion.300 = (f32[4,16,16,12]{3,2,1,0:T(8,128)}, f32[4,16,16,12]{3,2,1,0:T(8,128)}, f32[4,16,16,12]{3,2,1,0:T(8,128)}, f32[4,16,16,12]{3,2,1,0:T(8,128)}, f32[4...) fusion(bf16[4,16,16,12,64]{4,3,2,1,0:T(8,128)(2,1)} %reshape.49, ...), kind=kLoop, calls=%fused_computation.625 | loop fusion | flops 32083968 | bytes 25853952
  1365.1 16.1 fusion.391
  1395.7 11.1 scatter-add.421
  1807.7 12.8 reshape.5394
  1937.8 11.0 scatter-add.340
  2349.7 13.0 reshape.5393
  2407.0 14.9 collective-permute-done.4
  2436.5 155.5 %convert_reduce_fusion.1 = (f32[12,64]{1,0:T(8,128)}, bf16[4,16,16,12,64]{4,3,2,1,0:T(8,128)(2,1)}) fusion(bf16[4,16,16,12,64]{4,3,0,2,1:T(8,128)(2,1)} %get-tuple-element.1910, f32[4,16,16,12]{3,2,1,0:T(8,128)} %copy.972, bf16[4,16,16,12,64]{4,3,0,2,1:T(8,128)(2,1)} %get-tuple-element.1863, f32[4,16,16,12]{3,2,1,0:T(8,128)} %copy.971, ...), kind=kLoop, calls=%fused_computation.714 | loop fusion | flops 118750464 | bytes 81116160 | tf_op jit(solution)/shard_map/reduce_sum | solution.py:340
  2601.7 61.9 %all-reduce.3 = (bf16[4,12,64]{2,1,0:T(8,128)(2,1)S(1)}, bf16[4,12,64]{2,1,0:T(8,128)(2,1)}) all-reduce(f32[4,12,64]{2,1,0:T(8,128)} %bitcast.943, f32[4,12,64]{2,1,0:T(8,128)} %bitcast.944), channel_id=1, replica_groups=mesh['dp'=2,'row'=4,'col'=4] {'row','col'}, use_global_device_ids=true, to_apply=%region_25.26 | all-reduce | flops 6144 | bytes 36864 | tf_op jit(solution)/shard_map/psum | solution.py:329
  2691.2 11.1 fusion.625
  2736.8 38.8 %all-gather.2 = f32[64,12,64]{2,1,0:T(8,128)S(1)} all-gather(f32[4,12,64]{2,1,0:T(8,128)S(1)} %bitcast.942), channel_id=4, replica_groups=mesh['dp'=2,'row'=4,'col'=4] {'row','col'}, dimensions={0}, use_global_device_ids=true | all-gather | bytes 208896 | tf_op jit(solution)/shard_map/all_gather | solution.py:29
  2776.3 32.7 %all-gather.4 = f32[16,4,12]{2,1,0:T(4,128)S(1)} all-gather(f32[1,4,12]{2,1,0:T(4,128)S(1)} %bitcast.946), channel_id=3, replica_groups=mesh['dp'=2,'row'=4,'col'=4] {'row','col'}, dimensions={0}, use_global_device_ids=true | all-gather | bytes 3264 | tf_op jit(solution)/shard_map/all_gather | solution.py:29
  2809.0 29.4 all-gather.3
  2840.5 41.6 %while.121 = (s32[]{:T(128)}, f32[4,12]{1,0:T(4,128)}, f32[4,12]{1,0:T(4,128)S(1)}, f32[4,12,64]{2,1,0:T(8,128)}, f32[16,4,12]{2,1,0:T(4,128)}, /*index=5*/f32[1...) while((s32[]{:T(128)}, f32[4,12]{1,0:T(4,128)}, f32[4,12]{1,0:T(4,128)S(1)}, ...), condition=%wide.region_10.11_spmd, body=%wide.region_9.10_spmd.sunk | while | flops 9509 | bytes 38927 | solution.py:34
  2918.3 99.6 %reduce-scatter.21.cloned.1.call-done = f32[192,768]{1,0:T(8,128)} async-done(((f32[3072,768]{1,0:T(8,128)}), f32[192,768]{1,0:T(8,128)}) %reduce-scatter.21.cloned.1.call-update) | async-done | bytes 589840 | tf_op jit(solution)/shard_map/reduce_scatter | solution.py:364
  3024.5 43.4 %all-reduce.2 = (f32[768]{0:T(1024)}, f32[768]{0:T(1024)}, f32[768]{0:T(1024)}, f32[768]{0:T(1024)}, f32[768]{0:T(1024)}, /*index=5*/f32[12,50]{0,1:T(8,128)}, f...) all-reduce(f32[768]{0:T(1024)} %get-tuple-element.1694, ...), channel_id=1, replica_groups=mesh['dp'=2,'row'=4,'col'=4] {'dp','row','col'}, use_global_device_ids=true, to_apply=%region_37.38 | all-reduce | flops 12120 | bytes 96960 | tf_op jit(solution)/shard_map/psum | solution.py:372
  3073.2 10.9 reduce-scatter.23.cloned.1.call-done
  (1217 shorter events, 1795.9 us)
Async XLA Ops:
  7.2 2891.4 %reduce-scatter.13.cloned.1.call-start = ((), (), s32[]{:S(2)}) async-start(), calls=%async_computation.10 | async-start | bytes 2506752 | tf_op jit(solution)/shard_map/reduce_scatter | solution.py:362
  26.9 34.3 %collective-permute-start = (bf16[4,3,16,1536]{3,0,2,1:T(4,128)(2,1)}, bf16[4,3,16,1536]{3,0,2,1:T(4,128)(2,1)}, u32[]{:S(2)}, u32[]{:S(2)}) collective-permute-start(bf16[4,3,16,1536]{3,0,2,1:T(4,128)(2,1)} %copy.1911), channel_id=1, source_target_pairs={{0,4},{4,8},{8,12},{1,5},{5,9},{9,13},{2,6},{6,10},{10,14},{3,7},{... | collective-permute-start | bytes 1769480 | tf_op jit(solution)/shard_map/ppermute | solution.py:22
  31.4 35.9 %collective-permute-start.1 = (bf16[4,3,16,1536]{3,0,2,1:T(4,128)(2,1)}, bf16[4,3,16,1536]{3,0,2,1:T(4,128)(2,1)}, u32[]{:S(2)}, u32[]{:S(2)}) collective-permute-start(bf16[4,3,16,1536]{3,0,2,1:T(4,128)(2,1)} %copy.1912), channel_id=1, source_target_pairs={{4,0},{8,4},{12,8},{5,1},{9,5},{13,9},{6,2},{10,6},{14,10},{7,3},{... | collective-permute-start | bytes 1769480 | tf_op jit(solution)/shard_map/ppermute | solution.py:23
  69.2 22.2 collective-permute-start.2
  73.5 22.5 collective-permute-start.3
  115.1 84.4 %slice-start = ((s8[7929856]{0:T(1024)(128)(4,1)}), s8[3735552]{0:T(1024)(128)(4,1)S(1)}, s32[]{:S(2)}) async-start(s8[7929856]{0:T(1024)(128)(4,1)} %bitcast.927), calls=%async_computation.16 | async-start | bytes 7471104
  147.3 52.2 %slice-start.1 = ((s8[7929856]{0:T(1024)(128)(4,1)}), s8[4194304]{0:T(1024)(128)(4,1)S(1)}, s32[]{:S(2)}) async-start(s8[7929856]{0:T(1024)(128)(4,1)} %bitcast.927), calls=%async_computation.17 | async-start | bytes 8388608
  460.2 40.2 %copy-start.259 = (pred[16,16]{1,0:T(8,128)(4,1)S(1)}, pred[16,16]{1,0:T(8,128)(4,1)}, u32[]{:S(2)}) copy-start(pred[16,16]{1,0:T(8,128)(4,1)} %get-tuple-element.1955) | copy-start | bytes 772
  462.5 39.6 %copy-start.258 = (pred[16,16]{1,0:T(8,128)(4,1)S(1)}, pred[16,16]{1,0:T(8,128)(4,1)}, u32[]{:S(2)}) copy-start(pred[16,16]{1,0:T(8,128)(4,1)} %get-tuple-element.1954) | copy-start | bytes 772
  597.4 84.4 %slice-start.2 = ((s8[7929856]{0:T(1024)(128)(4,1)}), s8[3735552]{0:T(1024)(128)(4,1)S(1)}, s32[]{:S(2)}) async-start(s8[7929856]{0:T(1024)(128)(4,1)} %bitcast.929), calls=%async_computation.18 | async-start | bytes 7471104
  629.6 52.2 %slice-start.3 = ((s8[7929856]{0:T(1024)(128)(4,1)}), s8[4194304]{0:T(1024)(128)(4,1)S(1)}, s32[]{:S(2)}) async-start(s8[7929856]{0:T(1024)(128)(4,1)} %bitcast.929), calls=%async_computation.19 | async-start | bytes 8388608
  819.5 166.0 %copy-start.226 = (f32[768]{0:T(1024)S(1)}, f32[768]{0:T(1024)}, u32[]{:S(2)}) copy-start(f32[768]{0:T(1024)} %param.232) | copy-start | bytes 9220
  819.5 166.0 %copy-start.239 = (f32[768]{0:T(1024)S(1)}, f32[768]{0:T(1024)}, u32[]{:S(2)}) copy-start(f32[768]{0:T(1024)} %param.241) | copy-start | bytes 9220
  991.0 66.3 %copy-start.5 = (f32[1024,768]{1,0:T(8,128)}, f32[1024,768]{1,0:T(8,128)S(1)}, u32[]{:S(2)}) copy-start(f32[1024,768]{1,0:T(8,128)S(1)} %get-tuple-element.1702) | copy-start | bytes 9437188
  991.0 66.3 %copy-start.217 = (f32[1024]{0:T(1024)}, f32[1024]{0:T(1024)S(1)}, u32[]{:S(2)}) copy-start(f32[1024]{0:T(1024)S(1)} %broadcast_multiply_fusion.6) | copy-start | bytes 12292
  991.5 65.7 %copy-start.219 = (f32[1024]{0:T(1024)}, f32[1024]{0:T(1024)S(1)}, u32[]{:S(2)}) copy-start(f32[1024]{0:T(1024)S(1)} %add_rsqrt_fusion.1) | copy-start | bytes 12292
  1128.4 48.7 %copy-start.16 = (f32[4,16,16,12]{3,2,1,0:T(8,128)S(1)}, f32[4,16,16,12]{3,2,1,0:T(8,128)}, u32[]{:S(2)}) copy-start(f32[4,16,16,12]{3,2,1,0:T(8,128)} %copy.821) | copy-start | bytes 147460
  2383.2 38.7 %collective-permute-start.4 = (f32[4,22,3,1536]{3,0,2,1:T(4,128)}, f32[4,22,3,1536]{3,0,2,1:T(4,128)}, u32[]{:S(2)}, u32[]{:S(2)}) collective-permute-start(f32[4,22,3,1536]{3,0,2,1:T(4,128)} %get-tuple-element.1706), channel_id=1, source_target_pairs={{0,1},{1,2},{2,3},{4,5},{5,6},{6,7},{8,9},{9,10},{10,11},{12,13},{... | collective-permute-start | bytes 4866056 | tf_op jit(solution)/shard_map/ppermute | solution.py:12
  2387.9 39.4 %collective-permute-start.5 = (f32[4,22,3,1536]{3,0,2,1:T(4,128)}, f32[4,22,3,1536]{3,0,2,1:T(4,128)}, u32[]{:S(2)}, u32[]{:S(2)}) collective-permute-start(f32[4,22,3,1536]{3,0,2,1:T(4,128)} %get-tuple-element.1705), channel_id=1, source_target_pairs={{1,0},{2,1},{3,2},{5,4},{6,5},{7,6},{9,8},{10,9},{11,10},{13,12},{... | collective-permute-start | bytes 4866056 | tf_op jit(solution)/shard_map/ppermute | solution.py:12
  2404.7 498.0 %reduce-scatter.9.cloned.1.call-start = ((), (), s32[]{:S(2)}) async-start(), calls=%async_computation.8 | async-start | bytes 7520256 | tf_op jit(solution)/shard_map/reduce_scatter | solution.py:361
  2434.1 241.5 %collective-permute-start.6 = (f32[4,3,16,1536]{3,0,2,1:T(4,128)}, f32[4,3,16,1536]{3,0,2,1:T(4,128)}, u32[]{:S(2)}, u32[]{:S(2)}) collective-permute-start(f32[4,3,16,1536]{3,0,2,1:T(4,128)} %get-tuple-element.1812), channel_id=1, source_target_pairs={{0,4},{4,8},{8,12},{1,5},{5,9},{9,13},{2,6},{6,10},{10,14},{3,7},{... | collective-permute-start | bytes 3538952 | tf_op jit(solution)/shard_map/ppermute | solution.py:12
  2592.0 85.7 %collective-permute-start.7 = (f32[4,3,16,1536]{3,0,2,1:T(4,128)}, f32[4,3,16,1536]{3,0,2,1:T(4,128)}, u32[]{:S(2)}, u32[]{:S(2)}) collective-permute-start(f32[4,3,16,1536]{3,0,2,1:T(4,128)} %get-tuple-element.1811), channel_id=1, source_target_pairs={{4,0},{8,4},{12,8},{5,1},{9,5},{13,9},{6,2},{10,6},{14,10},{7,3},{... | collective-permute-start | bytes 3538952 | tf_op jit(solution)/shard_map/ppermute | solution.py:12
  2690.9 215.6 %reduce-scatter.17.cloned.1.call-start = ((), (), s32[]{:S(2)}) async-start(), calls=%async_computation.12 | async-start | bytes 10027008 | tf_op jit(solution)/shard_map/reduce_scatter | solution.py:363
  2702.3 315.6 %reduce-scatter.21.cloned.1.call-start = ((), (), s32[]{:S(2)}) async-start(), calls=%async_computation.14 | async-start | bytes 10027008 | tf_op jit(solution)/shard_map/reduce_scatter | solution.py:364
  2712.7 360.5 %reduce-scatter.15.cloned.1.call-start = ((), (), s32[]{:S(2)}) async-start(), calls=%async_computation.11 | async-start | bytes 221184 | tf_op jit(solution)/shard_map/reduce_scatter | solution.py:368
  2731.6 171.1 %copy-start.222 = (f32[768]{0:T(1024)S(1)}, f32[768]{0:T(1024)}, u32[]{:S(2)}) copy-start(f32[768]{0:T(1024)} %param.233) | copy-start | bytes 9220
  2775.6 64.8 %copy-start.213 = (f32[64,12,64]{2,1,0:T(8,128)}, f32[64,12,64]{2,1,0:T(8,128)S(1)}, u32[]{:S(2)}) copy-start(f32[64,12,64]{2,1,0:T(8,128)S(1)} %all-gather.2) | copy-start | bytes 589828
  2898.6 174.6 %reduce-scatter.11.cloned.1.call-start = ((), (), s32[]{:S(2)}) async-start(), calls=%async_computation.9 | async-start | bytes 663552 | tf_op jit(solution)/shard_map/reduce_scatter | solution.py:367
  2902.7 170.5 %reduce-scatter.19.cloned.1.call-start = ((), (), s32[]{:S(2)}) async-start(), calls=%async_computation.13 | async-start | bytes 884736 | tf_op jit(solution)/shard_map/reduce_scatter | solution.py:369
  2906.5 112.1 %copy-start.243 = (f32[1024]{0:T(1024)S(1)}, f32[1024]{0:T(1024)}, u32[]{:S(2)}) copy-start(f32[1024]{0:T(1024)} %copy-done.242) | copy-start | bytes 12292
  2906.5 112.1 %copy-start.245 = (f32[1024]{0:T(1024)S(1)}, f32[1024]{0:T(1024)}, u32[]{:S(2)}) copy-start(f32[1024]{0:T(1024)} %copy-done.244) | copy-start | bytes 12292
  2906.6 177.6 %reduce-scatter.23.cloned.1.call-start = ((), (), s32[]{:S(2)}) async-start(), calls=%async_computation.15 | async-start | bytes 884736 | tf_op jit(solution)/shard_map/reduce_scatter | solution.py:370
  (282 other events, 4029.1 us)
Sparse Core Ops, SparseCore 0:
  2404.8 66.9 reduce-scatter.12
  2691.0 94.0 reduce-scatter.8
  2789.2 113.0 reduce-scatter.16
  2906.7 111.1 reduce-scatter.20
  3020.5 10.2 reduce-scatter.14
  3033.5 13.7 reduce-scatter.10
  3050.2 15.4 reduce-scatter.18
  3068.5 15.6 reduce-scatter.22
where the time goes:
time: 3120 us; the launch traced here: 3090 us
  other arithmetic  1660 us (53%)
  local copies, waits for them, and re-layouts  881 us (28%)
  blocking collectives  206 us (7%)
  matrix products  171 us (5%)
  waiting for transfers between devices  138 us (4%)
    scatter-add x48, other arithmetic, shards(): value_grad_pad = value_grad_pad.at[:, shift_r:shift_r + tile_rows, shift_...  401 us
    scatter-add x48, other arithmetic, shards(): key_grad_pad = key_grad_pad.at[:, shift_r:shift_r + tile_rows, shift_c:sh...  401 us
    unnamed x57, other arithmetic  351 us
    slice x6, local copies, waits for them, and re-layouts, window_slice(): return array[:, shift_r:shift_r + tile_rows, shift_c:shift_c + tile_cols]  219 us
    convert_element_type x1, other arithmetic, shards(): attended = mixed.reshape(row_count, model_width).astype(jnp.bfloat16)  160 us
    reduce_sum x1, other arithmetic, shards(): grad_q_bias = jnp.sum(query_low.astype(jnp.float32), axis=0)  156 us
    dot_general x49, local copies, waits for them, and re-layouts, shards(): jnp.einsum('pijhd,pijhd->pijh', grad_mixed, value_part, preferred_element...  112 us
    dot_general x49, local copies, waits for them, and re-layouts, shards(): jnp.einsum('pijhd,pijhd->pijh', query_four, key_part, preferred_element_t...  112 us
  transfers between devices with their start and end apart: 16, of which 6 were waited for; matrix products, arithmetic and copies ran while one was open for 13% of the time, Pallas kernels for 0%

commit v1 on v0

v1 whole, which is shorter than its diff:
```python
import functools
import math

import jax
import jax.numpy as jnp
import numpy as np
from jax import lax
from jax.experimental import pallas as pl
from jax.experimental.pallas import tpu as pltpu
from jax.sharding import PartitionSpec as P

F32 = jnp.float32
BF16 = jnp.bfloat16
NEG = -1e30
REACH = 3
SPAN = 7
BAND = 4
SIDE = 8
LANES = 128
FLAG = 1024.0
EPS = 1e-06
MIB = 1 << 20


def dot(a, b):
    return jnp.dot(a, b, preferred_element_type=F32)


def dot_t(a, b):
    return lax.dot_general(a, b, (((1,), (1,)), ((), ())), preferred_element_type=F32)


def dot_0(a, b):
    return lax.dot_general(a, b, (((0,), (0,)), ((), ())), preferred_element_type=F32)


def split3(x):
    hi = x.astype(BF16)
    rest = x - hi.astype(F32)
    mid = rest.astype(BF16)
    low = (rest - mid.astype(F32)).astype(BF16)
    return hi, mid, low


def norm_parts(x):
    c = x - jnp.mean(x, axis=-1, keepdims=True)
    inv = lax.rsqrt(jnp.mean(c * c, axis=-1, keepdims=True) + EPS)
    return c * inv, inv


def norm_pull(e, unit, inv):
    return inv * (
        e
        - jnp.mean(e, axis=-1, keepdims=True)
        - unit * jnp.mean(e * unit, axis=-1, keepdims=True)
    )


def unmask(x, emb):
    return jnp.where(x > FLAG / 2, emb, x)


class Geometry:
    def __init__(self, pages, rows, cols, width, heads):
        self.pages, self.rows, self.cols = pages, rows, cols
        self.width, self.heads = width, heads
        self.head = width // heads
        self.lanes = 256
        self.stack = self.lanes // self.head
        self.groups = width // self.lanes
        self.own = rows * cols
        self.edge = REACH * cols
        self.side = (rows + 2 * REACH) * SIDE
        self.halo = 2 * self.edge + self.side + 16
        self.bands = rows // BAND
        self.band = BAND * cols
        self.main = (BAND + 2 * REACH) * cols
        self.flank = (BAND + 2 * REACH) * SIDE
        self.slots = self.main + self.flank + 16
        self.cls_at = self.main + self.flank
        slot = np.arange(self.slots)
        r = np.where(slot < self.main, slot // cols, (slot - self.main) // SIDE)
        s = (slot - self.main) % SIDE
        c = np.where(
            slot < self.main,
            slot % cols,
            np.where(s < REACH, s - REACH, np.where(s < 2 * REACH, cols + s - REACH, -1000)),
        )
        is_cls = slot >= self.cls_at
        r = np.where(is_cls, -1000, r)
        c = np.where(is_cls, -1000, c)
        self.slot_row, self.slot_col = r, c
        q = np.arange(self.band)
        a = r[None, :] - (q // cols)[:, None]
        b = c[None, :] - (q % cols)[:, None] + REACH
        ok = (a >= 0) & (a < SPAN) & (b >= 0) & (b < SPAN)
        offset = np.where(ok, a * SPAN + b, -1)
        mirror = np.where(ok, SPAN * SPAN - 1 - offset, -1)
        offset[:, self.cls_at] = SPAN * SPAN
        self.offset = offset.astype(np.int32)
        self.mirror = mirror.astype(np.int32)
        fold = np.full((cols, self.slots), -1, np.int32)
        for i in range(cols):
            for lane in range(SPAN * cols):
                d = lane % cols - i + REACH
                if 0 <= d < SPAN:
                    fold[i, lane] = lane // cols * SPAN + d
            for lane in range(SPAN * SIDE):
                s1 = lane % SIDE
                if s1 < 2 * REACH:
                    col = s1 - REACH if s1 < REACH else cols + s1 - REACH
                    d = col - i + REACH
                    if 0 <= d < SPAN:
                        fold[i, self.main + lane] = lane // SIDE * SPAN + d
            fold[i, self.cls_at] = SPAN * SPAN
        self.fold = fold.T.copy()
        lane = np.arange(self.lanes) // self.head
        self.head_mask = (np.arange(16)[:, None] == lane[None, :]).astype(np.float32)
        stat = np.zeros((self.groups, 16, LANES), np.float32)
        for g in range(self.groups):
            for h in range(self.stack):
                for part in range(3):
                    stat[g, h, 16 * part + g * self.stack + h] = -1.0
                    stat[g, 8 + h, 48 + 16 * part + g * self.stack + h] = -1.0
        self.stat_mask = stat
        self.to_head = (np.arange(width)[:, None] // self.head == np.arange(LANES)[None, :]).astype(
            np.float32
        )

    def block(self, own, halo, b):
        lo, hi = b * self.band, b * self.band + self.main
        e, o = self.edge, self.own
        parts = []
        if lo < e:
            parts.append(halo[lo : min(hi, e)])
        parts.append(own[max(lo - e, 0) : min(hi - e, o)])
        if hi > e + o:
            parts.append(halo[e + max(lo - e - o, 0) : e + hi - e - o])
        at = 2 * e + b * BAND * SIDE
        parts.append(halo[at : at + self.flank])
        parts.append(halo[2 * e + self.side : 2 * e + self.side + 16])
        return jnp.concatenate(parts, axis=0)

    def stacked(self, x, mask):
        return jnp.concatenate([x * mask[h : h + 1] for h in range(self.stack)], axis=0)

    def unstacked(self, r):
        rows = r.shape[0] // self.stack
        lane = lax.broadcasted_iota(jnp.int32, (rows, self.lanes), 1) // self.head
        out = r[(self.stack - 1) * rows :]
        for h in range(self.stack - 1):
            out = jnp.where(lane == h, r[h * rows : (h + 1) * rows], out)
        return out


def full(shape):
    return pl.BlockSpec(shape, lambda *_: (0,) * len(shape))


def params(limit, sem=1):
    return pltpu.CompilerParams(
        dimension_semantics=("arbitrary",) * sem, vmem_limit_bytes=limit * MIB
    )


def bias_body(geo, table, off_ref, mir_ref, a_ref, b_ref):
    def one(index_ref, out_ref):
        def rows(i, carry):
            at = pl.multiple_of(i * 8, 8)
            index = index_ref[pl.ds(at, 8), :]
            acc = [jnp.full((8, geo.slots), NEG, F32) for _ in range(geo.heads)]
            for o in range(SPAN * SPAN + 1):
                hit = index == o
                for h in range(geo.heads):
                    acc[h] = jnp.where(hit, table[h, o], acc[h])
            for h in range(geo.heads):
                g, k = divmod(h, geo.stack)
                out_ref[g, pl.ds(k * geo.band + at, 8), :] = acc[h]
            return carry

        lax.fori_loop(0, geo.band // 8, rows, 0)

    one(off_ref, a_ref)
    one(mir_ref, b_ref)


def bias_tables(geo, rel_table):
    shape = jax.ShapeDtypeStruct((geo.groups, geo.stack * geo.band, geo.slots), F32)
    return pl.pallas_call(
        functools.partial(bias_body, geo),
        out_shape=(shape, shape),
        in_specs=[pl.BlockSpec(memory_space=pltpu.SMEM)]
        + [pl.BlockSpec(memory_space=pltpu.VMEM)] * 2,
        out_specs=[pl.BlockSpec(memory_space=pltpu.VMEM)] * 2,
        name="bias_tables",
    )(rel_table, jnp.asarray(geo.offset), jnp.asarray(geo.mirror))


def qkv_body(x_ref, w_ref, vec_ref, bias_ref, o_ref):
    x = unmask(x_ref[...].astype(F32), vec_ref[0:1])
    unit, _ = norm_parts(x)
    normed = (unit * vec_ref[1:2] + vec_ref[2:3]).astype(BF16)
    o_ref[...] = (dot(normed, w_ref[...]) + bias_ref[0:1]).astype(BF16)


def qkv_call(x, w, vec, bias, tile):
    n, d = x.shape
    m = w.shape[1]
    return pl.pallas_call(
        qkv_body,
        out_shape=jax.ShapeDtypeStruct((n, m), BF16),
        grid=(n // tile,),
        in_specs=[
            pl.BlockSpec((tile, d), lambda i: (i, 0)),
            full((d, m)),
            full(vec.shape),
            full(bias.shape),
        ],
        out_specs=pl.BlockSpec((tile, m), lambda i: (i, 0)),
        compiler_params=params(40),
        cost_estimate=pl.CostEstimate(
            flops=2 * n * d * m, transcendentals=n, bytes_accessed=2 * (n * d + d * m + n * m)
        ),
        name="qkv",
    )(x, w, vec, bias)


def attend_body(
    geo, q_ref, k_ref, v_ref, hq_ref, hk_ref, hv_ref, bias_ref, ok_ref, hm_ref, hmf_ref,
    o_ref, lse_ref, cls_ref,
):
    g = pl.program_id(1)
    scale = BF16(1.0 / math.sqrt(geo.head))
    hm = hm_ref[...]
    q, k, v = q_ref[0], k_ref[0], v_ref[0]
    hk, hv = hk_ref[0], hv_ref[0]
    lane = lax.broadcasted_iota(jnp.int32, (geo.band, LANES), 1)

    @pl.when(g == 0)
    def _():
        lse_ref[...] = jnp.zeros_like(lse_ref)

    for b in range(geo.bands):
        rows = slice(b * geo.band, (b + 1) * geo.band)
        qs = geo.stacked(q[rows] * scale, hm)
        s = dot_t(qs, geo.block(k, hk, b)) + bias_ref[g] + ok_ref[b : b + 1]
        top = jnp.max(s, axis=-1, keepdims=True)
        e = jnp.exp(s - top)
        total = jnp.sum(e, axis=-1, keepdims=True)
        p = (e * (1.0 / total)).astype(BF16)
        o_ref[0, rows, :] = geo.unstacked(dot(p, geo.block(v, hv, b))).astype(BF16)
        lse = top + jnp.log(total)
        acc = lse_ref[0, rows, :]
        for h in range(geo.stack):
            acc = jnp.where(
                lane == g * geo.stack + h, lse[h * geo.band : (h + 1) * geo.band], acc
            )
        lse_ref[0, rows, :] = acc
    at = 2 * geo.edge + geo.side
    qc = jnp.broadcast_to(hq_ref[0, at : at + 1, :] * scale, (16, geo.lanes)) * hm
    s = dot_t(qc, k)
    top = jnp.max(s, axis=-1, keepdims=True)
    e = jnp.exp(s - top)
    total = jnp.sum(e, axis=-1, keepdims=True)
    hmf = hmf_ref[...]
    acc = sum(dot(part, v) for part in split3(e))
    cls_ref[0, 0:1, :] = jnp.sum(acc * hmf, axis=0, keepdims=True)
    cls_ref[0, 1:2, :] = jnp.sum(top * hmf, axis=0, keepdims=True)
    cls_ref[0, 2:3, :] = jnp.sum(total * hmf, axis=0, keepdims=True)
    cls_ref[0, 3:8, :] = jnp.zeros((5, geo.lanes), F32)


def lane_spec(rows, lanes, first):
    return pl.BlockSpec((1, rows, lanes), lambda p, g: (p, 0, first + g))


def attend_call(geo, own, halo, bias, ok, hm, hmf):
    G = geo.groups
    mm = 2 * geo.pages * G * geo.bands * 256 * 256 * 256
    return pl.pallas_call(
        functools.partial(attend_body, geo),
        out_shape=(
            jax.ShapeDtypeStruct((geo.pages, geo.own, geo.width), BF16),
            jax.ShapeDtypeStruct((geo.pages, geo.own, LANES), F32),
            jax.ShapeDtypeStruct((geo.pages, 8, geo.width), F32),
        ),
        grid=(geo.pages, G),
        in_specs=[lane_spec(geo.own, geo.lanes, i * G) for i in range(3)]
        + [lane_spec(geo.halo, geo.lanes, i * G) for i in range(3)]
        + [full(bias.shape), full(ok.shape), full(hm.shape), full(hmf.shape)],
        out_specs=[
            lane_spec(geo.own, geo.lanes, 0),
            pl.BlockSpec((1, geo.own, LANES), lambda p, g: (p, 0, 0)),
            lane_spec(8, geo.lanes, 0),
        ],
        compiler_params=params(40, 2),
        cost_estimate=pl.CostEstimate(
            flops=2 * mm, transcendentals=geo.pages * G * geo.bands * 65536, bytes_accessed=16 * MIB
        ),
        name="attend",
    )(own, own, own, halo, halo, halo, bias, ok, hm, hmf)


def mlp_body(
    tile, steps, att_ref, x_ref, og_ref, lse_ref, wout_ref, vec_ref, upb_ref, wup_ref, wdn_ref,
    toh_ref, out_ref, gmx_ref, gres_ref, dwup_ref, dwdn_ref, dwout_ref, vg_ref, dub_ref,
    n2, n2t, gm, branch, resid, mlp, dn2, act, dh,
):
    step = pl.program_id(0)
    n, d = n2.shape
    row = lambda i: vec_ref[i : i + 1]
    tiles = n // tile

    @pl.when(step == 0)
    def _():
        def one(t, carry):
            rows = pl.ds(pl.multiple_of(t * tile, tile), tile)
            br = dot(att_ref[rows, :], wout_ref[...]) + row(3)
            branch[rows, :] = br
            x = unmask(x_ref[rows, :].astype(F32), row(0))
            res = x + row(4) * br
            resid[rows, :] = res
            unit, _ = norm_parts(res)
            n2[rows, :] = (unit * row(5) + row(6)).astype(BF16)
            gm[rows, :] = (row(8) * og_ref[rows, :].astype(F32)).astype(BF16)
            mlp[rows, :] = jnp.zeros((tile, d), F32)
            dn2[rows, :] = jnp.zeros((tile, d), F32)
            return carry

        lax.fori_loop(0, tiles, one, 0)
        n2t[...] = n2[...].T
        vg_ref[...] = jnp.zeros_like(vg_ref)

    wup, wdn = wup_ref[...], wdn_ref[...]
    upb = upb_ref[0:1]

    def one(t, total):
        rows = pl.ds(pl.multiple_of(t * tile, tile), tile)
        h = dot(n2[rows, :], wup) + upb
        da = dot_t(gm[rows, :], wdn)
        cdf = 0.5 * (1.0 + lax.erf(h * math.sqrt(0.5)))
        pdf = jnp.exp(-0.5 * h * h) * (1.0 / math.sqrt(2.0 * math.pi))
        a = (h * cdf).astype(BF16)
        g = (da * (cdf + h * pdf)).astype(BF16)
        act[rows, :] = a
        dh[rows, :] = g
        mlp[rows, :] += dot(a, wdn)
        dn2[rows, :] += dot_t(g, wup)
        return total + jnp.sum(g.astype(F32), axis=0, keepdims=True)

    total = lax.fori_loop(0, tiles, one, jnp.zeros((1, wup.shape[1]), F32))
    dub_ref[...] = jnp.broadcast_to(total, dub_ref.shape)
    dwup_ref[...] = dot(n2t[...], dh[...]).astype(BF16)
    dwdn_ref[...] = dot_0(act[...], gm[...]).astype(BF16)

    @pl.when(step == steps - 1)
    def _():
        def one(t, carry):
            rows = pl.ds(pl.multiple_of(t * tile, tile), tile)
            add = lambda i, v: vg_ref.__setitem__(
                (slice(i, i + 1), slice(None)),
                vg_ref[i : i + 1] + jnp.sum(v, axis=0, keepdims=True),
            )
            res = resid[rows, :]
            og = og_ref[rows, :].astype(F32)
            mo = mlp[rows, :] + row(7)
            out_ref[rows, :] = (res + row(8) * mo).astype(BF16)
            add(0, og * mo)
            add(1, gm[rows, :].astype(F32))
            unit, inv = norm_parts(res)
            gn = dn2[rows, :]
            add(2, gn * unit)
            add(3, gn)
            gr = og + norm_pull(gn * row(5), unit, inv)
            gres_ref[rows, :] = gr
            add(4, gr * branch[rows, :])
            gb = (row(4) * gr).astype(BF16)
            add(5, gb.astype(F32))
            n2[rows, :] = gb
            mix = dot_t(gb, wout_ref[...]).astype(BF16)
            gmx_ref[rows, 0:d] = mix
            prod = mix.astype(F32) * att_ref[rows, :].astype(F32)
            toh = toh_ref[...]
            delta = sum(dot(part, toh) for part in split3(prod))
            packed = jnp.zeros((tile, LANES), F32)
            for i, part in enumerate(split3(lse_ref[rows, :]) + split3(delta)):
                part = part.astype(F32)
                packed += part if i == 0 else pltpu.roll(part, 16 * i, 1)
            gmx_ref[rows, d : d + LANES] = packed.astype(BF16)
            return carry

        lax.fori_loop(0, tiles, one, 0)
        dwout_ref[...] = dot_0(att_ref[...], n2[...]).astype(BF16)


def mlp_call(att, x, og, lse, w_out, vec, up_bias, w_up, w_down, to_head, chunk=256, tile=256):
    n, d = x.shape
    ff = w_up.shape[1]
    steps = ff // chunk
    hold = lambda shape: pl.BlockSpec(
        shape, lambda c: (0,) * len(shape), pipeline_mode=pl.Buffered(1)
    )
    return pl.pallas_call(
        functools.partial(mlp_body, tile, steps),
        out_shape=(
            jax.ShapeDtypeStruct((n, d), BF16),
            jax.ShapeDtypeStruct((n, d + LANES), BF16),
            jax.ShapeDtypeStruct((n, d), F32),
            jax.ShapeDtypeStruct((d, ff), BF16),
            jax.ShapeDtypeStruct((ff, d), BF16),
            jax.ShapeDtypeStruct((d, d), BF16),
            jax.ShapeDtypeStruct((8, d), F32),
            jax.ShapeDtypeStruct((8, ff), F32),
        ),
        grid=(steps,),
        in_specs=[
            hold((n, d)),
            hold((n, d)),
            hold((n, d)),
            hold((n, LANES)),
            hold((d, d)),
            hold(vec.shape),
            pl.BlockSpec((1, chunk), lambda c: (0, c)),
            pl.BlockSpec((d, chunk), lambda c: (0, c)),
            pl.BlockSpec((chunk, d), lambda c: (c, 0)),
            hold(to_head.shape),
        ],
        out_specs=[
            hold((n, d)),
            hold((n, d + LANES)),
            hold((n, d)),
            pl.BlockSpec((d, chunk), lambda c: (0, c)),
            pl.BlockSpec((chunk, d), lambda c: (c, 0)),
            hold((d, d)),
            hold((8, d)),
            pl.BlockSpec((8, chunk), lambda c: (0, c)),
        ],
        scratch_shapes=[
            pltpu.VMEM((n, d), BF16),
            pltpu.VMEM((d, n), BF16),
            pltpu.VMEM((n, d), BF16),
            pltpu.VMEM((n, d), F32),
            pltpu.VMEM((n, d), F32),
            pltpu.VMEM((n, d), F32),
            pltpu.VMEM((n, d), F32),
            pltpu.VMEM((n, chunk), BF16),
            pltpu.VMEM((n, chunk), BF16),
        ],
        compiler_params=params(56),
        cost_estimate=pl.CostEstimate(
            flops=2 * n * d * (6 * ff + 3 * d),
            transcendentals=2 * n * ff,
            bytes_accessed=2 * (8 * d * ff // 2 + 10 * n * d),
        ),
        name="mlp",
    )(att, x, og, lse, w_out, vec, up_bias, w_up, w_down, to_head)


def query_grad_body(
    geo, q_ref, k_ref, v_ref, hk_ref, hv_ref, gm_ref, st_ref, bias_ref, ok_ref, hm_ref, sm_ref,
    dq_ref, rel_ref,
):
    g, page = pl.program_id(0), pl.program_id(1)
    scale = 1.0 / math.sqrt(geo.head)
    hm = hm_ref[...]
    sm = sm_ref[g]
    q, k, v, gm, st = q_ref[0], k_ref[0], v_ref[0], gm_ref[0], st_ref[0]
    hk, hv = hk_ref[0], hv_ref[0]
    ones = jnp.ones((geo.slots, LANES), BF16)

    @pl.when(page == 0)
    def _():
        rel_ref[...] = jnp.zeros_like(rel_ref)

    for b in range(geo.bands):
        rows = slice(b * geo.band, (b + 1) * geo.band)
        kb = geo.block(k, hk, b)
        vb = geo.block(v, hv, b)
        qs = geo.stacked(q[rows] * BF16(scale), hm)
        gs = geo.stacked(gm[rows], hm)
        ql = geo.stacked(st[rows], sm[0:8])
        gl = geo.stacked(st[rows], sm[8:16])
        s = dot_t(qs, kb) + dot_t(ql, ones) + bias_ref[g] + ok_ref[b : b + 1]
        ds = jnp.exp(s) * (dot_t(gs, vb) + dot_t(gl, ones))
        rel_ref[0] += ds
        dl = (ds * scale).astype(BF16)
        dq_ref[0, rows, :] = geo.unstacked(dot(dl, kb)).astype(BF16)


def query_grad_call(geo, own, halo, gmx, bias, ok, hm, sm):
    G = geo.groups
    spec = lambda rows, first: pl.BlockSpec(
        (1, rows, geo.lanes), lambda g, p: (p, 0, first * G + g)
    )
    mm = 2 * geo.pages * G * geo.bands * 256 * 256 * 256
    return pl.pallas_call(
        functools.partial(query_grad_body, geo),
        out_shape=(
            jax.ShapeDtypeStruct((geo.pages, geo.own, geo.width), BF16),
            jax.ShapeDtypeStruct(bias.shape, F32),
        ),
        grid=(G, geo.pages),
        in_specs=[
            spec(geo.own, 0),
            spec(geo.own, 1),
            spec(geo.own, 2),
            spec(geo.halo, 1),
            spec(geo.halo, 2),
            spec(geo.own, 0),
            pl.BlockSpec((1, geo.own, LANES), lambda g, p: (p, 0, geo.width // LANES)),
            full(bias.shape),
            full(ok.shape),
            full(hm.shape),
            full(sm.shape),
        ],
        out_specs=[
            spec(geo.own, 0),
            pl.BlockSpec((1,) + bias.shape[1:], lambda g, p: (g, 0, 0)),
        ],
        compiler_params=params(40, 2),
        cost_estimate=pl.CostEstimate(
            flops=3 * mm, transcendentals=geo.pages * G * geo.bands * 65536, bytes_accessed=16 * MIB
        ),
        name="query_grad",
    )(own, own, own, halo, halo, gmx, gmx, bias, ok, hm, sm)


def key_grad_body(
    geo, q_ref, k_ref, v_ref, hq_ref, hk_ref, hv_ref, gm_ref, hgm_ref, st_ref, hst_ref, bias_ref,
    ok_ref, hm_ref, hmf_ref, sm_ref, ct_ref, dk_ref, dv_ref, cls_ref,
):
    g = pl.program_id(1)
    scale = 1.0 / math.sqrt(geo.head)
    hm = hm_ref[...]
    sm = sm_ref[g]
    q, k, v, gm, st = q_ref[0], k_ref[0], v_ref[0], gm_ref[0], st_ref[0]
    hq, hgm, hst = hq_ref[0], hgm_ref[0], hst_ref[0]
    spread = lambda m: jnp.concatenate(
        [jnp.broadcast_to(m[h : h + 1], (geo.band, LANES)) for h in range(geo.stack)], axis=0
    )
    kl, vl = spread(sm[0:8]), spread(sm[8:16])
    for b in range(geo.bands):
        rows = slice(b * geo.band, (b + 1) * geo.band)
        qb = geo.block(q, hq, b)
        gb = geo.block(gm, hgm, b)
        sb = geo.block(st, hst, b)
        ks = geo.stacked(k[rows] * BF16(scale), hm)
        vs = geo.stacked(v[rows], hm)
        s = dot_t(ks, qb) + dot_t(kl, sb) + bias_ref[g] + ok_ref[b : b + 1]
        p = jnp.exp(s)
        ds = p * (dot_t(vs, gb) + dot_t(vl, sb))
        dv_ref[0, rows, :] = geo.unstacked(dot(p.astype(BF16), gb)).astype(BF16)
        dk_ref[0, rows, :] = geo.unstacked(dot((ds * scale).astype(BF16), qb)).astype(BF16)
    at = 2 * geo.edge + geo.side
    kc = jnp.broadcast_to(hk_ref[0, at : at + 1, :] * BF16(scale), (16, geo.lanes)) * hm
    vc = jnp.broadcast_to(hv_ref[0, at : at + 1, :], (16, geo.lanes)) * hm
    zero = jnp.zeros((8, LANES), BF16)
    s = dot_t(kc, q) + dot_t(jnp.concatenate([sm[0:8], zero], 0), st) + ct_ref[g]
    p = jnp.exp(s)
    ds = p * (dot_t(vc, gm) + dot_t(jnp.concatenate([sm[8:16], zero], 0), st))
    hmf = hmf_ref[...]
    dkc = dot((ds * scale).astype(BF16), q)
    dvc = dot(p.astype(BF16), gm)
    cls_ref[0, 0:1, :] = jnp.sum(dkc * hmf, axis=0, keepdims=True)
    cls_ref[0, 1:2, :] = jnp.sum(dvc * hmf, axis=0, keepdims=True)
    cls_ref[0, 2:8, :] = jnp.zeros((6, geo.lanes), F32)


def key_grad_call(geo, own, halo, gmx, hgmx, bias, ok, hm, hmf, sm, ct):
    G = geo.groups
    stat = lambda rows: pl.BlockSpec((1, rows, LANES), lambda p, g: (p, 0, geo.width // LANES))
    mm = 2 * geo.pages * G * geo.bands * 256 * 256 * 256
    return pl.pallas_call(
        functools.partial(key_grad_body, geo),
        out_shape=(
            jax.ShapeDtypeStruct((geo.pages, geo.own, geo.width), BF16),
            jax.ShapeDtypeStruct((geo.pages, geo.own, geo.width), BF16),
            jax.ShapeDtypeStruct((geo.pages, 8, geo.width), F32),
        ),
        grid=(geo.pages, G),
        in_specs=[lane_spec(geo.own, geo.lanes, i * G) for i in range(3)]
        + [lane_spec(geo.halo, geo.lanes, i * G) for i in range(3)]
        + [
            lane_spec(geo.own, geo.lanes, 0),
            lane_spec(geo.halo, geo.lanes, 0),
            stat(geo.own),
            stat(geo.halo),
        ]
        + [full(a.shape) for a in (bias, ok, hm, hmf, sm, ct)],
        out_specs=[
            lane_spec(geo.own, geo.lanes, 0),
            lane_spec(geo.own, geo.lanes, 0),
            lane_spec(8, geo.lanes, 0),
        ],
        compiler_params=params(40, 2),
        cost_estimate=pl.CostEstimate(
            flops=4 * mm, transcendentals=geo.pages * G * geo.bands * 65536, bytes_accessed=20 * MIB
        ),
        name="key_grad",
    )(own, own, own, halo, halo, halo, gmx, hgmx, gmx, hgmx, bias, ok, hm, hmf, sm, ct)


def table_body(geo, acc_ref, fold_ref, o_ref):
    lane = lax.broadcasted_iota(jnp.int32, (geo.cols, geo.slots), 1)
    heads = []
    for g in range(geo.groups):
        for h in range(geo.stack):
            x = acc_ref[g, h * geo.band : (h + 1) * geo.band, :]
            parts = [x[i * geo.cols : (i + 1) * geo.cols] for i in range(BAND)]
            main, side, plain = parts[0], parts[0], parts[0]
            for i in range(1, BAND):
                main = main + pltpu.roll(parts[i], geo.slots - i * geo.cols, 1)
                side = side + pltpu.roll(parts[i], geo.slots - i * SIDE, 1)
                plain = plain + parts[i]
            z = jnp.where(lane < SPAN * geo.cols, main, jnp.where(lane < geo.cls_at, side, plain))
            heads.append(z)
    pad = [jnp.zeros((geo.cols, geo.slots), F32)] * (16 - geo.heads)
    z = jnp.stack(heads + pad, axis=0)
    total = jnp.zeros((16, LANES), F32)
    which = lax.broadcasted_iota(jnp.int32, (geo.slots, LANES), 1)
    for i in range(geo.cols):
        pick = jnp.where(fold_ref[:, i : i + 1] == which, 1.0, 0.0).astype(BF16)
        for part in split3(z[:, i, :]):
            total += dot(part, pick)
    o_ref[...] = total


def table_call(geo, acc):
    return pl.pallas_call(
        functools.partial(table_body, geo),
        out_shape=jax.ShapeDtypeStruct((16, LANES), F32),
        compiler_params=pltpu.CompilerParams(vmem_limit_bytes=40 * MIB),
        name="table_grad",
    )(acc, jnp.asarray(geo.fold))


def qkv_weight_body(
    tile, x_ref, dq_ref, dk_ref, dv_ref, c_ref, cg_ref, vec_ref, dw_ref, vg_ref, nt, ct
):
    which = pl.program_id(0)
    n, d = x_ref.shape

    @pl.when(which == 0)
    def _():
        def one(t, carry):
            rows = pl.ds(pl.multiple_of(t * tile, tile), tile)
            unit, _ = norm_parts(unmask(x_ref[rows, :].astype(F32), vec_ref[0:1]))
            nt[:, rows] = (unit * vec_ref[1:2] + vec_ref[2:3]).astype(BF16).T
            return carry

        lax.fori_loop(0, n // tile, one, 0, unroll=True)
        unit, _ = norm_parts(c_ref[...].astype(F32))
        ct[...] = unit * vec_ref[1:2] + vec_ref[2:3]
        vg_ref[...] = jnp.zeros_like(vg_ref)

    def go(ref, extra, bias_row):
        grad = ref[...]
        if extra is None:
            dw_ref[...] = dot(nt[...], grad).astype(BF16)
        else:
            dw_ref[...] = (dot(nt[...], grad) + dot_0(ct[...].astype(BF16), extra)).astype(BF16)
        if bias_row is not None:
            total = jnp.sum(grad.astype(F32), axis=0, keepdims=True)
            if extra is not None:
                total = total + jnp.sum(extra.astype(F32), axis=0, keepdims=True)
            vg_ref[bias_row : bias_row + 1] = total

    @pl.when(which == 0)
    def _():
        go(dq_ref, None, 0)

    @pl.when(which == 1)
    def _():
        go(dk_ref, cg_ref[:, 0:d], None)

    @pl.when(which == 2)
    def _():
        go(dv_ref, cg_ref[:, d : 2 * d], 1)


def qkv_weight_call(x, dq, dk, dv, cls_rows, cls_grad, vec, tile=256):
    n, d = x.shape
    return pl.pallas_call(
        functools.partial(qkv_weight_body, tile),
        out_shape=(
            jax.ShapeDtypeStruct((d, 3 * d), BF16),
            jax.ShapeDtypeStruct((8, d), F32),
        ),
        grid=(3,),
        in_specs=[full(a.shape) for a in (x, dq, dk, dv, cls_rows, cls_grad, vec)],
        out_specs=[pl.BlockSpec((d, d), lambda i: (0, i)), full((8, d))],
        scratch_shapes=[pltpu.VMEM((d, n), BF16), pltpu.VMEM((16, d), F32)],
        compiler_params=params(48),
        cost_estimate=pl.CostEstimate(
            flops=2 * n * d * 3 * d, transcendentals=n, bytes_accessed=2 * (4 * n * d + 3 * d * d)
        ),
        name="qkv_weight",
    )(x, dq, dk, dv, cls_rows, cls_grad, vec)


def token_grad_body(
    x_ref, dq_ref, dk_ref, dv_ref, gres_ref, w_ref, c_ref, cg_ref, vec_ref, dt_ref, dc_ref, vg_ref
):
    d = x_ref.shape[1]
    wq, wk, wv = w_ref[:, 0:d], w_ref[:, d : 2 * d], w_ref[:, 2 * d : 3 * d]
    gain = vec_ref[1:2]

    @pl.when(pl.program_id(0) == 0)
    def _():
        unit, inv = norm_parts(c_ref[...].astype(F32))
        gn = dot_t(cg_ref[:, 0:d], wk) + dot_t(cg_ref[:, d : 2 * d], wv)
        dc_ref[...] = norm_pull(gn * gain, unit, inv)
        vg_ref[...] = jnp.zeros_like(vg_ref)
        vg_ref[1:2] = jnp.sum(gn * unit, axis=0, keepdims=True)
        vg_ref[2:3] = jnp.sum(gn, axis=0, keepdims=True)

    raw = x_ref[...].astype(F32)
    masked = raw > FLAG / 2
    unit, inv = norm_parts(jnp.where(masked, vec_ref[0:1], raw))
    gn = dot_t(dq_ref[...], wq) + dot_t(dk_ref[...], wk) + dot_t(dv_ref[...], wv)
    gs = gres_ref[...] + norm_pull(gn * gain, unit, inv)
    dt_ref[...] = jnp.where(masked, 0.0, gs)
    vg_ref[0:1] += jnp.sum(jnp.where(masked, gs, 0.0), axis=0, keepdims=True)
    vg_ref[1:2] += jnp.sum(gn * unit, axis=0, keepdims=True)
    vg_ref[2:3] += jnp.sum(gn, axis=0, keepdims=True)


def token_grad_call(x, dq, dk, dv, gres, w_qkv, cls_rows, cls_grad, vec, tile=256):
    n, d = x.shape
    rows = pl.BlockSpec((tile, d), lambda i: (i, 0))
    return pl.pallas_call(
        token_grad_body,
        out_shape=(
            jax.ShapeDtypeStruct((n, d), F32),
            jax.ShapeDtypeStruct((16, d), F32),
            jax.ShapeDtypeStruct((8, d), F32),
        ),
        grid=(n // tile,),
        in_specs=[rows] * 5 + [full(a.shape) for a in (w_qkv, cls_rows, cls_grad, vec)],
        out_specs=[rows, full((16, d)), full((8, d))],
        compiler_params=params(48),
        cost_estimate=pl.CostEstimate(
            flops=2 * n * d * 3 * d, transcendentals=n, bytes_accessed=2 * (8 * n * d + 3 * d * d)
        ),
        name="token_grad",
    )(x, dq, dk, dv, gres, w_qkv, cls_rows, cls_grad, vec)


def passed_along(value, axis, steps):
    count = lax.axis_size(axis)
    first, last = max(0, -steps), min(count, count - steps)
    return lax.ppermute(value, axis, [(i, i + steps) for i in range(first, last)])


def halo_of(x, rows, cols):
    pages, width = x.shape[0], x.shape[-1]
    tile = x.reshape(pages, rows, cols, width)
    top = passed_along(tile[:, rows - REACH :], "row", 1)
    bottom = passed_along(tile[:, :REACH], "row", -1)
    tall = lambda cut: jnp.concatenate([cut(top), cut(tile), cut(bottom)], axis=1)
    left = passed_along(tall(lambda a: a[:, :, cols - REACH :]), "col", 1)
    right = passed_along(tall(lambda a: a[:, :, :REACH]), "col", -1)
    gap = jnp.zeros((pages, rows + 2 * REACH, SIDE - 2 * REACH, width), x.dtype)
    side = jnp.concatenate([left, right, gap], axis=2)
    flat = lambda a: a.reshape(pages, -1, width)
    return [flat(top), flat(bottom), flat(side)]


def summed(value, axis):
    count, step = lax.axis_size(axis), 1
    while step < count:
        value = value + lax.ppermute(value, axis, [(i, i ^ step) for i in range(count)])
        step *= 2
    return value


def shards(
    tokens, cls_token, patch_mask, loss_mask, mask_emb, ln1_gain, ln1_bias, w_qkv, q_bias, v_bias,
    rel_table, w_out, out_bias, scale_attn, ln2_gain, ln2_bias, w_up, up_bias, w_down, down_bias,
    scale_mlp, out_grad,
):
    pages, rows, cols, width = tokens.shape
    heads = rel_table.shape[0]
    geo = Geometry(pages, rows, cols, width, heads)
    count = pages * rows * cols
    grid_rows, grid_cols = rows * lax.axis_size("row"), cols * lax.axis_size("col")

    vec = jnp.concatenate(
        [
            a[None]
            for a in (
                mask_emb, ln1_gain, ln1_bias, out_bias, scale_attn, ln2_gain, ln2_bias, down_bias,
                scale_mlp,
            )
        ]
        + [jnp.zeros((7, width), F32)],
        axis=0,
    )
    qkv_bias = jnp.concatenate([q_bias, jnp.zeros((width,), F32), v_bias])[None]
    qkv_bias = jnp.broadcast_to(qkv_bias, (8, 3 * width))
    hm = jnp.asarray(geo.head_mask, BF16)
    hmf = jnp.asarray(geo.head_mask, F32)
    sm = jnp.asarray(geo.stat_mask, BF16)
    to_head = jnp.asarray(geo.to_head, BF16)
    class_bias = jnp.zeros((geo.groups, 16), F32)
    class_bias = class_bias.at[:, : geo.stack].set(
        rel_table[:, SPAN * SPAN].reshape(geo.groups, geo.stack)
    )
    class_bias = jnp.broadcast_to(class_bias[:, :, None], (geo.groups, 16, geo.own))

    first_row = lax.axis_index("row") * rows - REACH
    first_col = lax.axis_index("col") * cols
    at_row = first_row + BAND * np.arange(8)[:, None] + geo.slot_row[None, :]
    at_col = first_col + geo.slot_col[None, :]
    inside = (at_row >= 0) & (at_row < grid_rows) & (at_col >= 0) & (at_col < grid_cols)
    inside = inside | (np.arange(geo.slots) >= geo.cls_at)[None, :]
    ok = jnp.where(inside, 0.0, NEG).astype(F32)

    flag = jnp.asarray(FLAG, BF16)
    masked = (patch_mask == 1)[..., None]
    marked = jnp.where(masked, flag, tokens)
    counted = (patch_mask * loss_mask == 1)[..., None]
    out_g = jnp.where(counted, out_grad, jnp.zeros((), BF16)).reshape(count, width)
    x = marked.reshape(count, width)

    bias_a, bias_b = bias_tables(geo, rel_table)
    own = qkv_call(x, w_qkv, vec, qkv_bias, geo.own).reshape(pages, geo.own, 3 * width)
    cls_block = jnp.concatenate(
        [cls_token[:, None], jnp.zeros((pages, 15, width), BF16)], axis=1
    )
    halo_x = jnp.concatenate(halo_of(marked, rows, cols) + [cls_block], axis=1)
    halo = qkv_call(
        halo_x.reshape(pages * geo.halo, width), w_qkv, vec, qkv_bias, geo.halo
    ).reshape(pages, geo.halo, 3 * width)

    att, lse, cls_part = attend_call(geo, own, halo, bias_a, ok, hm, hmf)
    att = att.reshape(count, width)
    out, gmx, gres, d_up, d_down, d_wout, vg_mlp, d_upb = mlp_call(
        att, x, out_g, lse.reshape(count, LANES), w_out, vec, up_bias[None], w_up, w_down, to_head
    )
    gmx = gmx.reshape(pages, geo.own, width + LANES)
    dq, rel_acc = query_grad_call(geo, own, halo, gmx, bias_a, ok, hm, sm)
    halo_g = jnp.concatenate(
        halo_of(gmx, rows, cols) + [jnp.zeros((pages, 16, width + LANES), BF16)], axis=1
    )
    dk, dv, cls_grad = key_grad_call(
        geo, own, halo, gmx, halo_g, bias_b, ok, hm, hmf, sm, class_bias
    )
    d_table = table_call(geo, rel_acc)
    dq, dk, dv = (a.reshape(count, width) for a in (dq, dk, dv))
    cls_rows = jnp.concatenate([cls_token, jnp.zeros((16 - pages, width), BF16)], axis=0)
    cls_low = jnp.concatenate([cls_grad[:, 0], cls_grad[:, 1]], axis=-1).astype(BF16)
    cls_low = jnp.concatenate([cls_low, jnp.zeros((16 - pages, 2 * width), BF16)], axis=0)
    d_qkv, vg_qkv = qkv_weight_call(x, dq, dk, dv, cls_rows, cls_low, vec)
    d_tok, d_cls, vg_tok = token_grad_call(x, dq, dk, dv, gres, w_qkv, cls_rows, cls_low, vec)

    tile_axes = ("row", "col")

    def scattered(grad):
        part = lax.psum_scatter(grad, tile_axes, scatter_dimension=0, tiled=True)
        return lax.psum_scatter(part, "dp", scatter_dimension=1, tiled=True).astype(F32)

    weight_grads = [scattered(g) for g in (d_qkv, d_wout, d_up, d_down)]

    slots = lax.axis_size("row") * lax.axis_size("col")
    mine = lax.axis_index("row") * lax.axis_size("col") + lax.axis_index("col")
    here = (jnp.arange(slots) == mine)[:, None, None, None]
    everyone = lax.psum(jnp.where(here, cls_part[None, :, :3], 0.0), tile_axes)
    cls_in = cls_token.astype(F32)
    cls_qkv = halo[:, 2 * geo.edge + geo.side].astype(F32)
    cq, ck, cv = jnp.split(cls_qkv, 3, axis=-1)
    own_score = jnp.sum((cq * ck).reshape(pages, heads, geo.head), axis=-1) / math.sqrt(geo.head)
    own_score = jnp.repeat(own_score, geo.head, axis=-1)
    tops = everyone[:, :, 1]
    top = jnp.maximum(jnp.max(tops, axis=0), own_score)
    weight = jnp.exp(tops - top)
    own_weight = jnp.exp(own_score - top)
    total = jnp.sum(everyone[:, :, 2] * weight, axis=0) + own_weight
    mixed = (jnp.sum(everyone[:, :, 0] * weight, axis=0) + own_weight * cv) / total
    cls_branch = dot(mixed.astype(BF16), w_out) + out_bias
    cls_res = cls_in + scale_attn * cls_branch
    cls_unit, _ = norm_parts(cls_res)
    cls_two = (cls_unit * ln2_gain + ln2_bias).astype(BF16)
    cls_act = jax.nn.gelu(dot(cls_two, w_up) + up_bias, approximate=False).astype(BF16)
    out_cls = (cls_res + scale_mlp * (dot(cls_act, w_down) + down_bias)).astype(BF16)

    table_rows = jnp.pad(d_table[:heads].reshape(-1), (0, 2 * width - heads * LANES)).reshape(2, width)
    vectors = jnp.concatenate(
        [
            d_cls[:pages],
            vg_tok[0:3],
            vg_qkv[0:2],
            vg_mlp[0:6],
            d_upb[0].reshape(-1, width),
            table_rows,
        ],
        axis=0,
    )
    vectors = summed(summed(vectors, "row"), "col")
    d_cls = vectors[:pages]
    v = summed(vectors[pages:], "dp")
    ups = w_up.shape[1] // width
    d_rel = v[11 + ups :].reshape(-1)[: heads * LANES].reshape(heads, LANES)[:, : SPAN * SPAN + 1]
    return (
        out.reshape(tokens.shape),
        out_cls,
        d_tok.reshape(tokens.shape),
        d_cls,
        *weight_grads,
        v[0],
        v[1],
        v[2],
        v[3],
        v[4],
        d_rel,
        v[10],
        v[9],
        v[7],
        v[8],
        v[11 : 11 + ups].reshape(-1),
        v[6],
        v[5],
    )


def solution(mesh):
    tile = P("dp", "row", "col", None)
    flat = P("dp", "row", "col")
    weights = P(("row", "col"), "dp")
    return jax.shard_map(
        shards,
        mesh=mesh,
        in_specs=(tile, P("dp", None), flat, flat) + (P(),) * 17 + (tile,),
        out_specs=(tile, P("dp", None), tile, P("dp", None)) + (weights,) * 4 + (P(),) * 13,
        check_vma=False,
    )
```

time: 3120 us -> 595 us (0.19)
  other arithmetic: 1660 us -> 18.9 us
  local copies, waits for them, and re-layouts: 881 us -> 36 us
  blocking collectives: 206 us -> 0 us
  waiting for transfers between devices: 138 us -> 321 us
  Pallas kernels: 0 us -> 167 us
  matrix products: 171 us -> 6.28 us
    scatter-add x100 -> x0, other arithmetic: 812 us -> none  [the longest x48 401 us: shards(): value_grad_pad = value_grad_pad.at[:, shift_r:shift_r + tile_rows, shift_...]
    unnamed x57 -> x1, other arithmetic: 351 us -> 0.01 us
    slice x24 -> x25, local copies, waits for them, and re-layouts: 252 us -> 5.34 us  [the longest x1 1.14 us: halo_of(): top = passed_along(tile[:, rows - REACH:], 'row', 1)]
    mul x101 -> x0, local copies, waits for them, and re-layouts: 226 us -> none  [the longest x49 110 us: shards(): dscore_low[..., shift_r * 7 + shift_c, None].astype(jnp.float32)]
    dot_general x101 -> x0, local copies, waits for them, and re-layouts: 225 us -> none  [the longest x49 112 us: shards(): jnp.einsum('pijhd,pijhd->pijh', grad_mixed, value_part, preferred_element...]
    reduce_sum x17 -> x3, other arithmetic: 214 us -> 0.39 us  [the longest x1 0.19 us: norm_parts(): inv = lax.rsqrt(jnp.mean(c * c, axis=-1, keepdims=True) + EPS)]
    convert_element_type x10 -> x5, other arithmetic: 181 us -> 4.66 us  [the longest x4 3.73 us: scattered(): lax.psum_scatter(part, 'dp', scatter_dimension=1, tiled=True).astype(F32)]
    pallas_call x0 -> x10, Pallas kernels: none -> 167 us  [the longest x1 68.7 us: mlp_call(): pl.pallas_call(functools.partial(mlp_body, tile, steps), out_shape=(jax.S...]
  transfers between devices with their start and end apart: 16 -> 22, of which waited for: 6 -> 12; matrix products, arithmetic and copies ran while one was open for 13% -> 6% of each run, Pallas kernels for 0% -> 13%
where the time goes in v1:
time: 595 us; the launch traced here: 593 us
  waiting for transfers between devices  321 us (54%)
  Pallas kernels  167 us (28%)
  local copies, waits for them, and re-layouts  36 us (6%)
  starting transfers between devices  29.3 us (5%)
  other arithmetic  18.9 us (3%)
  between operations  15.3 us (3%)
  matrix products  6.28 us (1%)
    reduce_scatter x4, waiting for transfers between devices, scattered(): part = lax.psum_scatter(grad, tile_axes, scatter_dimension=0, tiled=True)  192 us
    psum x1, waiting for transfers between devices, shards(): everyone = lax.psum(jnp.where(here, cls_part[None, :, :3], 0.0), tile_axes)  71.4 us
    pallas_call x1, Pallas kernels, mlp_call(): pl.pallas_call(functools.partial(mlp_body, tile, steps), out_shape=(jax.S...  68.7 us
    unnamed x12, waiting for transfers between devices  34.9 us
    unnamed x133, local copies, waits for them, and re-layouts  25.1 us
    ppermute x8, starting transfers between devices, passed_along(): lax.ppermute(value, axis, [(i, i + steps) for i in range(first, last)])  23.1 us
    pallas_call x1, Pallas kernels, key_grad_call(): pl.pallas_call(functools.partial(key_grad_body, geo), out_shape=(jax.Shap...  21.9 us
    pallas_call x1, Pallas kernels, query_grad_call(): pl.pallas_call(functools.partial(query_grad_body, geo), out_shape=(jax.Sh...  17.9 us
  transfers between devices with their start and end apart: 22, of which 12 were waited for; matrix products, arithmetic and copies ran while one was open for 6% of the time, Pallas kernels for 13%

profile of v1, /device:TPU:0, one launch (start us, length us, event | category | flops | bytes accessed | tf_op | source)
XLA Modules:
  0.0 593.5 jit_solution(15679996955317511561)
XLA Ops:
  8.0 3.0 broadcast_select_fusion
  13.4 3.0 collective-permute-start
  17.3 8.3 %bias_tables.1 = (f32[3,256,256]{2,1,0:T(8,128)}, f32[3,256,256]{2,1,0:T(8,128)}) custom-call(f32[12,50]{1,0:T(8,128)} %table.1, s32[64,256]{1,0:T(8,128)} %constant.170.clone.off_ref, s32[64,256]{1,0:T(8,128)} %constant.171.clone.mir_ref), custom_call_target="tpu_custom_call" | custom-call | tf_op jit(solution)/shard_map/bias_tables/pallas_call | solution.py:189
  27.7 5.8 collective-permute-start.2
  35.6 5.2 qkv.2
  40.8 2.1 copy-done
  44.4 2.6 concatenate.50
  47.0 2.1 copy-done.17
  49.2 5.8 qkv.3
  55.0 17.3 %attend.1 = (bf16[4,256,768]{2,1,0:T(8,128)(2,1)S(1)}, f32[4,256,128]{2,1,0:T(8,128)S(1)}, f32[4,8,768]{2,1,0:T(8,128)S(1)}) custom-call(bf16[4,256,2304]{2,1,0:T(8,128)(2,1)S(1)} %bitcast.70, bf16[4,256,2304]{2,1,0:T(8,128)(2,1)S(1)} %bitcast.71, bf16[4,256,2304]{2,1,0:T(8,128)(2,1)S(1)} %bitcast.72, bf16[4,288,2304]{2,1,0:T(8,128)(2,1)S(1)} %bitcast.79, ...), custom_call_target="tpu_custom_call" | custom-call | flops 3221225472 | bytes 16777216 | tf_op jit(solution)/shard_map/attend/pallas_call | solution.py:280
  74.4 68.7 %mlp.1 = (bf16[1024,768]{1,0:T(8,128)(2,1)}, bf16[1024,896]{1,0:T(8,128)(2,1)}, f32[1024,768]{1,0:T(8,128)}, bf16[768,3072]{1,0:T(8,128)(2,1)}, bf16[3072,768]{1...) custom-call(bf16[1024,768]{1,0:T(8,128)(2,1)} %bitcast.106, ...), custom_call_target="tpu_custom_call" | custom-call | flops 32614907904 | bytes 34603008 | tf_op jit(solution)/shard_map/mlp/pallas_call | solution.py:403
  147.6 3.4 collective-permute-start.4
  155.9 5.7 collective-permute-start.6
  162.6 2.4 copy-done.1
  164.9 17.9 %query_grad.1 = (bf16[4,256,768]{2,1,0:T(8,128)(2,1)S(1)}, f32[3,256,256]{2,1,0:T(8,128)S(1)}) custom-call(bf16[4,256,2304]{2,1,0:T(8,128)(2,1)S(1)} %bitcast.73, bf16[4,256,2304]{2,1,0:T(8,128)(2,1)S(1)} %bitcast.74, bf16[4,256,2304]{2,1,0:T(8,128)(2,1)S(1)} %bitcast.75, bf16[4,288,2304]{2,1,0:T(8,128)(2,1)} %bitcast.82, bf16[4,288,2304]{2,1,0:T(8,128)(2,1)} %bitcast.83, ...), custom_call_target="tpu_custom_call" | custom-call | flops 4831838208 | bytes 16777216 | tf_op jit(solution)/shard_map/query_grad/pallas_call | solution.py:496
  183.1 2.6 maximum_maximum_fusion.1
  187.0 21.9 %key_grad.1 = (bf16[4,256,768]{2,1,0:T(8,128)(2,1)S(1)}, bf16[4,256,768]{2,1,0:T(8,128)(2,1)S(1)}, f32[4,8,768]{2,1,0:T(8,128)S(1)}) custom-call(bf16[4,256,2304]{2,1,0:T(8,128)(2,1)S(1)} %bitcast.76, bf16[4,256,2304]{2,1,0:T(8,128)(2,1)S(1)} %bitcast.77, bf16[4,256,2304]{2,1,0:T(8,128)(2,1)S(1)} %bitcast.78, bf16[4,288,2304]{2,1,0:T(8,128)(2,1)} %bitcast.84, ...), custom_call_target="tpu_custom_call" | custom-call | flops 6442450944 | bytes 20971520 | tf_op jit(solution)/shard_map/key_grad/pallas_call | solution.py:573
  210.3 8.9 %qkv_weight.1 = (bf16[768,2304]{1,0:T(8,128)(2,1)}, f32[8,768]{1,0:T(8,128)S(1)}) custom-call(bf16[1024,768]{1,0:T(8,128)(2,1)S(1)} %bitcast.96, bf16[1024,768]{1,0:T(8,128)(2,1)S(1)} %bitcast.100, bf16[1024,768]{1,0:T(8,128)(2,1)S(1)} %bitcast.102, bf16[1024,768]{1,0:T(8,128)(2,1)} %bitcast.104, bf16[16,768]{1,0:T(8,128)(2,1)S(1)} %concatenate.55.c_ref, ...), custom_call_target="tpu_custom_call" | custom-call | flops 3623878656 | bytes 9830400 | tf_op jit(solution)/shard_map/qkv_weight/pallas_call | solution.py:683
  226.0 71.4 %all-reduce.5.cloned.1.call-done = f32[16,4,3,768]{3,0,1,2:T(8,128)} async-done(((f32[16,4,3,768]{3,0,1,2:T(8,128)}), f32[16,4,3,768]{3,0,1,2:T(8,128)}) %all-reduce.5.cloned.1.call-update) | async-done | bytes 589840 | tf_op jit(solution)/shard_map/psum | solution.py:868
  298.5 69.8 %reduce-scatter.15.cloned.1.call-done = bf16[48,2304]{1,0:T(8,128)(2,1)} async-done(((bf16[768,2304]{1,0:T(8,128)(2,1)}), bf16[48,2304]{1,0:T(8,128)(2,1)}) %reduce-scatter.15.cloned.1.call-update) | async-done | bytes 221200 | tf_op jit(solution)/shard_map/reduce_scatter | solution.py:860
  373.3 11.4 %token_grad.1 = (f32[1024,768]{1,0:T(8,128)}, f32[16,768]{1,0:T(8,128)S(1)}, f32[8,768]{1,0:T(8,128)S(1)}) custom-call(bf16[1024,768]{1,0:T(8,128)(2,1)S(1)} %bitcast.97, bf16[1024,768]{1,0:T(8,128)(2,1)S(1)} %bitcast.101, bf16[1024,768]{1,0:T(8,128)(2,1)S(1)} %bitcast.103, bf16[1024,768]{1,0:T(8,128)(2,1)} %bitcast.105, ...), custom_call_target="tpu_custom_call" | custom-call | flops 3623878656 | bytes 16121856 | tf_op jit(solution)/shard_map/token_grad/pallas_call | solution.py:731
  385.2 61.3 %reduce-scatter.23.cloned.1.call-done = bf16[192,768]{1,0:T(8,128)(2,1)} async-done(((bf16[3072,768]{1,0:T(8,128)(2,1)}), bf16[192,768]{1,0:T(8,128)(2,1)}) %reduce-scatter.23.cloned.1.call-update) | async-done | bytes 294928 | tf_op jit(solution)/shard_map/reduce_scatter | solution.py:860
  449.7 3.6 collective-permute-done.9
  454.5 3.2 collective-permute-done.10
  457.7 2.2 collective-permute-start.11
  459.9 3.2 collective-permute-done.11
  464.6 60.7 %reduce-scatter.19.cloned.1.call-done = bf16[48,3072]{1,0:T(8,128)(2,1)} async-done(((bf16[768,3072]{1,0:T(8,128)(2,1)}), bf16[48,3072]{1,0:T(8,128)(2,1)}) %reduce-scatter.19.cloned.1.call-update) | async-done | bytes 294928 | tf_op jit(solution)/shard_map/reduce_scatter | solution.py:860
  525.4 5.9 fusion.4
  533.8 4.1 reduce-scatter.27.cloned.1.call-done
  539.6 15.9 %reduce-scatter.25.cloned.1.call-done = bf16[1152,48]{1,0:T(8,128)(2,1)} async-done(((bf16[2304,48]{1,0:T(8,128)(2,1)}), bf16[1152,48]{1,0:T(8,128)(2,1)}) %reduce-scatter.25.cloned.1.call-update) | async-done | bytes 110608
  557.3 13.7 %reduce-scatter.29.cloned.1.call-done = bf16[384,192]{1,0:T(8,128)(2,1)} async-done(((bf16[768,192]{1,0:T(8,128)(2,1)}), bf16[384,192]{1,0:T(8,128)(2,1)}) %reduce-scatter.29.cloned.1.call-update) | async-done | bytes 147472
  572.8 12.5 %reduce-scatter.21.cloned.1.call-done = bf16[48,1536]{1,0:T(8,128)(2,1)} async-done(((bf16[48,3072]{1,0:T(8,128)(2,1)}), bf16[48,1536]{1,0:T(8,128)(2,1)}) %reduce-scatter.21.cloned.1.call-update) | async-done | bytes 147472 | tf_op jit(solution)/shard_map/reduce_scatter | solution.py:861
  (268 shorter events, 52.4 us)
Async XLA Ops:
  7.2 214.4 %reduce-scatter.17.cloned.1.call-start = ((), (), s32[]{:S(2)}) async-start(), calls=%async_computation.10 | async-start | bytes 1253376 | tf_op jit(solution)/shard_map/reduce_scatter | solution.py:860
  12.1 13.6 %collective-permute-start.1 = (bf16[4,3,16,768]{3,2,1,0:T(8,128)(2,1)}, bf16[4,3,16,768]{3,2,1,0:T(8,128)(2,1)S(1)}, u32[]{:S(2)}, u32[]{:S(2)}) collective-permute-start(bf16[4,3,16,768]{3,2,1,0:T(8,128)(2,1)} %get-tuple-element.100), channel_id=1, source_target_pairs={{4,0},{8,4},{12,8},{5,1},{9,5},{13,9},{6,2},{10,6},{14,10},{7,3},{... | collective-permute-start | bytes 884744 | tf_op jit(solution)/shard_map/ppermute | solution.py:752
  13.4 12.5 %collective-permute-start = (bf16[4,3,16,768]{3,2,1,0:T(8,128)(2,1)}, bf16[4,3,16,768]{3,2,1,0:T(8,128)(2,1)S(1)}, u32[]{:S(2)}, u32[]{:S(2)}) collective-permute-start(bf16[4,3,16,768]{3,2,1,0:T(8,128)(2,1)} %get-tuple-element.101), channel_id=1, source_target_pairs={{0,4},{4,8},{8,12},{1,5},{5,9},{9,13},{2,6},{6,10},{10,14},{3,7},{... | collective-permute-start | bytes 884744 | tf_op jit(solution)/shard_map/ppermute | solution.py:752
  17.3 26.4 %copy-start.53 = (bf16[8]{0:T(256)(128)(2,1)}, bf16[8]{0:T(256)(128)(2,1)S(1)}, u32[]{:S(2)}) copy-start(bf16[8]{0:T(256)(128)(2,1)S(1)} %pad.22.clone) | copy-start | bytes 52
  26.2 16.7 %collective-permute-start.3 = (bf16[4,22,3,768]{3,1,2,0:T(8,128)(2,1)S(1)}, bf16[4,22,3,768]{3,1,2,0:T(8,128)(2,1)S(1)}, u32[]{:S(2)}, u32[]{:S(2)}) collective-permute-start(bf16[4,22,3,768]{3,1,2,0:T(8,128)(2,1)S(1)} %pad_maximum_fusion.3), channel_id=1, source_target_pairs={{1,0},{2,1},{3,2},{5,4},{6,5},{7,6},{9,8},{10,9},{11,10},{13,12},{... | collective-permute-start | bytes 1216520 | tf_op jit(solution)/shard_map/ppermute | solution.py:752
  27.7 15.8 %collective-permute-start.2 = (bf16[4,22,3,768]{3,1,2,0:T(8,128)(2,1)S(1)}, bf16[4,22,3,768]{3,1,2,0:T(8,128)(2,1)S(1)}, u32[]{:S(2)}, u32[]{:S(2)}) collective-permute-start(bf16[4,22,3,768]{3,1,2,0:T(8,128)(2,1)S(1)} %pad_maximum_fusion.2), channel_id=1, source_target_pairs={{0,1},{1,2},{2,3},{4,5},{5,6},{6,7},{8,9},{9,10},{10,11},{12,13},{... | collective-permute-start | bytes 1216520 | tf_op jit(solution)/shard_map/ppermute | solution.py:752
  74.4 69.5 %copy-start.35 = (f32[12,50]{1,0:T(8,128)S(1)}, f32[12,50]{1,0:T(8,128)}, u32[]{:S(2)}) copy-start(f32[12,50]{1,0:T(8,128)} %table.1) | copy-start | bytes 7204
  143.1 154.3 %all-reduce.5.cloned.1.call-start = ((), (), s32[]{:S(2)}) async-start(), calls=%async_computation.8 | async-start | bytes 1179648 | tf_op jit(solution)/shard_map/psum | solution.py:868
  146.1 6.0 %collective-permute-start.5 = (bf16[4,3,16,896]{3,0,2,1:T(4,128)(2,1)S(1)}, bf16[4,3,16,896]{3,0,2,1:T(4,128)(2,1)S(1)}, u32[]{:S(2)}, u32[]{:S(2)}) collective-permute-start(bf16[4,3,16,896]{3,0,2,1:T(4,128)(2,1)S(1)} %copy.140), channel_id=1, source_target_pairs={{4,0},{8,4},{12,8},{5,1},{9,5},{13,9},{6,2},{10,6},{14,10},{7,3},{... | collective-permute-start | bytes 1032200 | tf_op jit(solution)/shard_map/ppermute | solution.py:752
  147.6 4.6 collective-permute-start.4
  153.5 29.6 %collective-permute-start.7 = (bf16[4,22,3,896]{3,0,2,1:T(4,128)(2,1)}, bf16[4,22,3,896]{3,0,2,1:T(4,128)(2,1)}, u32[]{:S(2)}, u32[]{:S(2)}) collective-permute-start(bf16[4,22,3,896]{3,0,2,1:T(4,128)(2,1)} %pad_maximum_fusion.1), channel_id=1, source_target_pairs={{1,0},{2,1},{3,2},{5,4},{6,5},{7,6},{9,8},{10,9},{11,10},{13,12},{... | collective-permute-start | bytes 1419272 | tf_op jit(solution)/shard_map/ppermute | solution.py:752
  155.9 27.2 %collective-permute-start.6 = (bf16[4,22,3,896]{3,0,2,1:T(4,128)(2,1)}, bf16[4,22,3,896]{3,0,2,1:T(4,128)(2,1)}, u32[]{:S(2)}, u32[]{:S(2)}) collective-permute-start(bf16[4,22,3,896]{3,0,2,1:T(4,128)(2,1)} %pad_maximum_fusion), channel_id=1, source_target_pairs={{0,1},{1,2},{2,3},{4,5},{5,6},{6,7},{8,9},{9,10},{10,11},{12,13},{... | collective-permute-start | bytes 1419272 | tf_op jit(solution)/shard_map/ppermute | solution.py:752
  162.5 205.8 %reduce-scatter.15.cloned.1.call-start = ((), (), s32[]{:S(2)}) async-start(), calls=%async_computation.9 | async-start | bytes 3760128 | tf_op jit(solution)/shard_map/reduce_scatter | solution.py:860
  182.9 27.3 %copy-start.18 = (bf16[4,256,768]{2,1,0:T(8,128)(2,1)}, bf16[4,256,768]{2,1,0:T(8,128)(2,1)S(1)}, u32[]{:S(2)}) copy-start(bf16[4,256,768]{2,1,0:T(8,128)(2,1)S(1)} %get-tuple-element.62) | copy-start | bytes 4718596
  219.3 227.2 %reduce-scatter.23.cloned.1.call-start = ((), (), s32[]{:S(2)}) async-start(), calls=%async_computation.13 | async-start | bytes 5013504 | tf_op jit(solution)/shard_map/reduce_scatter | solution.py:860
  219.8 305.5 %reduce-scatter.19.cloned.1.call-start = ((), (), s32[]{:S(2)}) async-start(), calls=%async_computation.11 | async-start | bytes 5013504 | tf_op jit(solution)/shard_map/reduce_scatter | solution.py:860
  220.4 317.5 %reduce-scatter.27.cloned.1.call-start = ((), (), s32[]{:S(2)}) async-start(), calls=%async_computation.15 | async-start | bytes 294912
  223.4 332.1 %reduce-scatter.25.cloned.1.call-start = ((), (), s32[]{:S(2)}) async-start(), calls=%async_computation.14 | async-start | bytes 884736
  297.4 73.0 %copy-start.26 = (f32[16,4,3,768]{3,0,1,2:T(8,128)S(1)}, f32[16,4,3,768]{3,0,1,2:T(8,128)}, u32[]{:S(2)}) copy-start(f32[16,4,3,768]{3,0,1,2:T(8,128)} %all-reduce.5.cloned.1.call-done) | copy-start | bytes 1769476
  370.3 200.6 %reduce-scatter.29.cloned.1.call-start = ((), (), s32[]{:S(2)}) async-start(), calls=%async_computation.16 | async-start | bytes 589824
  373.3 75.1 %copy-start.25 = (bf16[768,768]{1,0:T(8,128)(2,1)S(1)}, bf16[768,768]{1,0:T(8,128)(2,1)}, u32[]{:S(2)}) copy-start(bf16[768,768]{1,0:T(8,128)(2,1)} %wout_ref.1) | copy-start | bytes 3538948
  385.0 140.3 %copy-start.40 = (f32[768]{0:T(1024)S(1)}, f32[768]{0:T(1024)}, u32[]{:S(2)}) copy-start(f32[768]{0:T(1024)} %param.49) | copy-start | bytes 9220
  385.0 140.3 %copy-start.42 = (f32[768]{0:T(1024)S(1)}, f32[768]{0:T(1024)}, u32[]{:S(2)}) copy-start(f32[768]{0:T(1024)} %param.50) | copy-start | bytes 9220
  385.1 140.3 %copy-start.44 = (f32[768]{0:T(1024)S(1)}, f32[768]{0:T(1024)}, u32[]{:S(2)}) copy-start(f32[768]{0:T(1024)} %param.54) | copy-start | bytes 9220
  385.1 140.3 %copy-start.46 = (f32[768]{0:T(1024)S(1)}, f32[768]{0:T(1024)}, u32[]{:S(2)}) copy-start(f32[768]{0:T(1024)} %param.55) | copy-start | bytes 9220
  385.1 140.3 %copy-start.47 = (f32[3072]{0:T(1024)S(1)}, f32[3072]{0:T(1024)}, u32[]{:S(2)}) copy-start(f32[3072]{0:T(1024)} %param.52) | copy-start | bytes 36868
  385.1 63.7 %collective-permute-start.8 = (f32[21,768]{1,0:T(8,128)S(1)}, f32[21,768]{1,0:T(8,128)S(1)}, u32[]{:S(2)}, u32[]{:S(2)}) collective-permute-start(f32[21,768]{1,0:T(8,128)S(1)} %concatenate.58), channel_id=1, source_target_pairs={{0,4},{4,0},{8,12},{12,8},{1,5},{5,1},{9,13},{13,9},{2,6},{6,2},{1... | collective-permute-start | bytes 193544 | tf_op jit(solution)/shard_map/ppermute | solution.py:772
  448.4 136.9 %reduce-scatter.21.cloned.1.call-start = ((), (), s32[]{:S(2)}) async-start(), calls=%async_computation.12 | async-start | bytes 442368 | tf_op jit(solution)/shard_map/reduce_scatter | solution.py:861
  448.9 4.4 collective-permute-start.9
  453.3 4.4 collective-permute-start.10
  457.7 5.3 collective-permute-start.11
  463.1 68.8 %collective-permute-start.12 = (f32[17,768]{1,0:T(8,128)S(1)}, f32[17,768]{1,0:T(8,128)S(1)}, u32[]{:S(2)}, u32[]{:S(2)}) collective-permute-start(f32[17,768]{1,0:T(8,128)S(1)} %slice.226), channel_id=1, source_target_pairs={{0,16},{16,0},{1,17},{17,1},{2,18},{18,2},{3,19},{19,3},{4,20},{20... | collective-permute-start | bytes 156680 | tf_op jit(solution)/shard_map/ppermute | solution.py:772
  (51 other events, 418.6 us)
Sparse Core Ops, SparseCore 0:
  143.2 60.1 reduce-scatter.16
  206.8 90.5 all-reduce.4
  301.3 66.9 reduce-scatter.14
  372.0 74.4 reduce-scatter.22
  450.6 74.5 reduce-scatter.18
  527.9 9.9 reduce-scatter.26
  540.2 15.2 reduce-scatter.24
  557.8 13.1 reduce-scatter.28
  573.2 12.0 reduce-scatter.20
